TPU v7x, 32 devices: a whole 2x2x4 slice. The times are simulated.
32 devices in a mesh: dp: 16 (over z, y, x), mp: 2 (over core).
Axes of the slice: x: 2, y: 2, z: 4, core: 2. Of those that a mesh axis runs over, the one named last changes fastest.
Arguments:
- tokens: bfloat16 [32768, 768], P(('dp', 'mp')), may hold values from -6 to 6
- w_query: bfloat16 [768, 768], P('dp', 'mp'), may hold values from -0.21875 to 0.21875
- w_key: bfloat16 [768, 768], P('dp', 'mp'), may hold values from -0.21875 to 0.21875
- w_value: bfloat16 [768, 768], P('dp', 'mp'), may hold values from -0.21875 to 0.21875
- w_out: bfloat16 [768, 768], P('mp', 'dp'), may hold values from -0.875 to 0.875
- w_gate: bfloat16 [768, 3072], P('dp', 'mp'), may hold values from -0.21875 to 0.21875
- w_up: bfloat16 [768, 3072], P('dp', 'mp'), may hold values from -0.21875 to 0.21875
- w_down: bfloat16 [3072, 768], P('mp', 'dp'), may hold values from -0.109375 to 0.109375
- attention_norm_gain: float32 [768], replicated, may hold values from 0.5 to 1.5
- feedforward_norm_gain: float32 [768], replicated, may hold values from 0.5 to 1.5
- block_seq: int32 [16, 32], P('dp'), may hold values from 0 to 31, as said below
- block_len: int32 [16, 32], P('dp'), may hold values from 0 to 64, as said below
- cotangent: bfloat16 [32768, 768], P(('dp', 'mp')), may hold values from -6 to 6
Outputs:
- output: bfloat16 [32768, 768], P(('dp', 'mp'))
- input_grad: bfloat16 [32768, 768], P(('dp', 'mp'))
- grad_w_query: float32 [768, 768], P('dp', 'mp')
- grad_w_key: float32 [768, 768], P('dp', 'mp')
- grad_w_value: float32 [768, 768], P('dp', 'mp')
- grad_w_out: float32 [768, 768], P('mp', 'dp')
- grad_w_gate: float32 [768, 3072], P('dp', 'mp')
- grad_w_up: float32 [768, 3072], P('dp', 'mp')
- grad_w_down: float32 [3072, 768], P('mp', 'dp')
- grad_gain_attn: float32 [768], replicated
- grad_gain_ffn: float32 [768], replicated
Inputs may be any that keep to these rules, and one draw needn't show every extreme that they name: `block_seq`: within each pack (aligned runs of 32 entries of a row) either every entry is 0, one document, or entry b of the pack is b, one query to a block; in every draw some pack holds a document and some pack holds queries. `block_len`: A query holds 8 to 64 valid rows, and one query of every query pack holds 64. A document of L rows, 64 <= L <= 2048, has 64 valid rows in its blocks before row L - L % 64, L % 64 in the next block and 0 after; in every draw some document holds 2048 rows.
All inputs are finite; a program needn't handle non-finite values.
Results may differ from a plain program's by a relative error of at most 0.02.
Values may be sent and summed in bfloat16 or wider, within the bound.
No kernel may reach another device: no remote copies, remote signals or barrier semaphores. Data moves between devices by JAX's collectives and lax.ppermute only.
A program may use at most 256 MiB of HBM per device.

v0:
```python
import math

import jax
import jax.numpy as jnp
from jax import lax
from jax.sharding import PartitionSpec as P

HEAD_DIM = 64
SEQ_MAX = 2048
QLEN = 64
PACKS = 1


EPS = 1e-05
ROPE_BASE = 1000.0


def block_layout(seq_row, len_row):
    blocks = SEQ_MAX // QLEN
    sequence = seq_row.reshape(PACKS, blocks)
    lengths = len_row.reshape(PACKS, blocks)
    earlier = jnp.sum((sequence[:, None, :] < sequence[:, :, None]).astype(jnp.int32), axis=2)
    inside = jnp.arange(SEQ_MAX, dtype=jnp.int32)
    row_seq = jnp.repeat(sequence, QLEN, axis=1)
    position = inside[None, :] - QLEN * jnp.repeat(earlier, QLEN, axis=1)
    key_valid = (inside % QLEN)[None, :] < jnp.repeat(lengths, QLEN, axis=1)
    return (row_seq, position, key_valid)


def rotary_tables(position):
    half = HEAD_DIM // 2
    ladder = jnp.arange(half, dtype=jnp.int32).astype(jnp.float32)
    inverse = jnp.exp(ladder * (-2.0 * math.log(ROPE_BASE) / HEAD_DIM))
    angle = position.astype(jnp.float32)[:, None] * inverse[None, :]
    return (jnp.cos(angle), jnp.sin(angle))


def rotate(value, cosine, sine):
    half = value.shape[-1] // 2
    first = value[..., :half]
    second = value[..., half:]
    cos_row = cosine[:, None, :]
    sin_row = sine[:, None, :]
    return jnp.concatenate(
        [first * cos_row - second * sin_row, second * cos_row + first * sin_row], axis=-1
    )


def rotate_back(upstream_gradient, cosine, sine):
    half = upstream_gradient.shape[-1] // 2
    first = upstream_gradient[..., :half]
    second = upstream_gradient[..., half:]
    cos_row = cosine[:, None, :]
    sin_row = sine[:, None, :]
    return jnp.concatenate(
        [first * cos_row + second * sin_row, second * cos_row - first * sin_row], axis=-1
    )


def layer_normalize(value):
    row_mean = jnp.mean(value, axis=-1, keepdims=True)
    centred = value - row_mean
    inverse_deviation = lax.rsqrt(jnp.mean(centred * centred, axis=-1, keepdims=True) + EPS)
    return (centred * inverse_deviation, inverse_deviation)


def layer_normalize_backward(upstream_gradient, normalized_input, inverse_deviation, norm_gain):
    scaled_rows = upstream_gradient * norm_gain
    return inverse_deviation * (
        scaled_rows
        - jnp.mean(scaled_rows, axis=-1, keepdims=True)
        - normalized_input * jnp.mean(scaled_rows * normalized_input, axis=-1, keepdims=True)
    )


def contract_rows(left, right):
    return lax.dot_general(
        left, right, (((0,), (0,)), ((), ())), preferred_element_type=jnp.float32
    )


def times_transposed(left, right):
    return lax.dot_general(
        left, right, (((1,), (1,)), ((), ())), preferred_element_type=jnp.float32
    )


def allowed_pairs(seq_block, seq_pack, valid_pack):
    return (seq_block[:, None] == seq_pack[None, :]) & valid_pack[None, :]


def attention_forward(query, keys, values, row_seq, key_valid):
    rows, heads, width = query.shape
    packs, length = row_seq.shape
    block = min(512, length)
    count = length // block
    scale = HEAD_DIM ** (-0.5)

    def one_pack(item):
        query_pack, key_pack, value_pack, seq_pack, valid_pack = item

        def one_block(piece):
            query_block, seq_block = piece
            allowed = allowed_pairs(seq_block, seq_pack, valid_pack)
            scores = (
                jnp.einsum(
                    "qhd,khd->hqk", query_block, key_pack, preferred_element_type=jnp.float32
                )
                * scale
            )
            scores = jnp.where(allowed[None], scores, -1e30)
            peak = jnp.max(scores, axis=-1, keepdims=True)
            expo = jnp.exp(scores - peak)
            total = jnp.sum(expo, axis=-1, keepdims=True)
            probs = (expo / total).astype(jnp.bfloat16)
            mixed = jnp.einsum(
                "hqk,khd->qhd", probs, value_pack, preferred_element_type=jnp.float32
            )
            return (mixed.astype(jnp.bfloat16), (peak + jnp.log(total))[..., 0])

        mixed, logsum = lax.map(one_block, (query_pack, seq_pack.reshape(count, block)))
        return (mixed.reshape(length, heads, width), logsum)

    mixed, logsum = lax.map(
        one_pack,
        (
            query.reshape(packs, count, block, heads, width),
            keys.reshape(packs, length, heads, width),
            values.reshape(packs, length, heads, width),
            row_seq,
            key_valid,
        ),
    )
    return (mixed.reshape(rows, heads * width), logsum)


def attention_backward(query, keys, values, grad_context, row_seq, key_valid, logsum):
    rows, heads, width = query.shape
    packs, length = row_seq.shape
    block = min(512, length)
    count = length // block
    scale = HEAD_DIM ** (-0.5)

    def one_pack(item):
        query_pack, key_pack, value_pack, grad_pack, seq_pack, valid_pack, logsum_pack = item

        def one_block(carry, piece):
            key_total, value_total = carry
            query_block, grad_block, seq_block, logsum_block = piece
            allowed = allowed_pairs(seq_block, seq_pack, valid_pack)
            scores = (
                jnp.einsum(
                    "qhd,khd->hqk", query_block, key_pack, preferred_element_type=jnp.float32
                )
                * scale
            )
            scores = jnp.where(allowed[None], scores, -1e30)
            probs = jnp.exp(scores - logsum_block[..., None])
            grad_probs = jnp.einsum(
                "qhd,khd->hqk", grad_block, value_pack, preferred_element_type=jnp.float32
            )
            delta = jnp.sum(probs * grad_probs, axis=-1, keepdims=True)
            grad_scores = (probs * (grad_probs - delta)).astype(jnp.bfloat16)
            grad_query = (
                jnp.einsum(
                    "hqk,khd->qhd", grad_scores, key_pack, preferred_element_type=jnp.float32
                )
                * scale
            )
            key_total = (
                key_total
                + jnp.einsum(
                    "hqk,qhd->khd", grad_scores, query_block, preferred_element_type=jnp.float32
                )
                * scale
            )
            value_total = value_total + jnp.einsum(
                "hqk,qhd->khd",
                probs.astype(jnp.bfloat16),
                grad_block,
                preferred_element_type=jnp.float32,
            )
            return ((key_total, value_total), grad_query)

        zeros = jnp.zeros((length, heads, width), jnp.float32)
        (key_grad, value_grad), query_grad = lax.scan(
            one_block,
            (zeros, zeros),
            (query_pack, grad_pack, seq_pack.reshape(count, block), logsum_pack),
        )
        return (query_grad.reshape(length, heads, width), key_grad, value_grad)

    query_grad, key_grad, value_grad = lax.map(
        one_pack,
        (
            query.reshape(packs, count, block, heads, width),
            keys.reshape(packs, length, heads, width),
            values.reshape(packs, length, heads, width),
            grad_context.reshape(packs, count, block, heads, width),
            row_seq,
            key_valid,
            logsum,
        ),
    )
    return (
        query_grad.reshape(rows, heads, width),
        key_grad.reshape(rows, heads, width),
        value_grad.reshape(rows, heads, width),
    )


def local(
    tokens,
    w_query,
    w_key,
    w_value,
    w_out,
    w_gate,
    w_up,
    w_down,
    attention_norm_gain,
    feedforward_norm_gain,
    block_seq,
    block_len,
    cotangent,
):
    row_seq, position, key_valid = block_layout(block_seq[0], block_len[0])
    cosine, sine = rotary_tables(position.reshape(-1))
    rows_all = lax.all_gather(tokens, "mp", axis=0, tiled=True)
    query_full, key_full, value_full, out_full = (
        lax.all_gather(w_query, "dp", axis=0, tiled=True),
        lax.all_gather(w_key, "dp", axis=0, tiled=True),
        lax.all_gather(w_value, "dp", axis=0, tiled=True),
        lax.all_gather(w_out, "dp", axis=1, tiled=True),
    )
    heads = query_full.shape[1] // HEAD_DIM
    rows_grp = rows_all.shape[0]

    def split_heads(value):
        return value.reshape(rows_grp, heads, HEAD_DIM)

    query = rotate(
        split_heads(jnp.dot(rows_all, query_full, preferred_element_type=jnp.float32)), cosine, sine
    ).astype(jnp.bfloat16)
    keys = rotate(
        split_heads(jnp.dot(rows_all, key_full, preferred_element_type=jnp.float32)), cosine, sine
    ).astype(jnp.bfloat16)
    values = split_heads(
        jnp.dot(rows_all, value_full, preferred_element_type=jnp.float32).astype(jnp.bfloat16)
    )
    context, logsum = attention_forward(query, keys, values, row_seq, key_valid)
    attention_output = lax.psum_scatter(
        jnp.dot(context, out_full, preferred_element_type=jnp.float32).astype(jnp.bfloat16),
        "mp",
        scatter_dimension=0,
        tiled=True,
    ).astype(jnp.float32)
    attention_normalized_input, attention_inverse_deviation = layer_normalize(
        tokens.astype(jnp.float32) + attention_output
    )
    hidden_state = attention_normalized_input * attention_norm_gain
    hidden_low = hidden_state.astype(jnp.bfloat16)
    gate_full, up_full, down_full = (
        lax.all_gather(w_gate, "dp", axis=0, tiled=True),
        lax.all_gather(w_up, "dp", axis=0, tiled=True),
        lax.all_gather(w_down, "dp", axis=1, tiled=True),
    )
    hidden_rows = lax.all_gather(hidden_low, "mp", axis=0, tiled=True)
    gate = jnp.dot(hidden_rows, gate_full, preferred_element_type=jnp.float32)
    up_value = jnp.dot(hidden_rows, up_full, preferred_element_type=jnp.float32)
    act = (gate * jax.nn.sigmoid(gate) * up_value).astype(jnp.bfloat16)
    branch_output = lax.psum_scatter(
        jnp.dot(act, down_full, preferred_element_type=jnp.float32).astype(jnp.bfloat16),
        "mp",
        scatter_dimension=0,
        tiled=True,
    ).astype(jnp.float32)
    feedforward_normalized_input, feedforward_inverse_deviation = layer_normalize(
        hidden_state + branch_output
    )
    output = (feedforward_normalized_input * feedforward_norm_gain).astype(jnp.bfloat16)
    output_gradient = cotangent.astype(jnp.float32)
    feedforward_gain_slice = jnp.sum(output_gradient * feedforward_normalized_input, axis=0)
    middle_gradient = layer_normalize_backward(
        output_gradient,
        feedforward_normalized_input,
        feedforward_inverse_deviation,
        feedforward_norm_gain,
    )
    grad_branch = lax.all_gather(middle_gradient.astype(jnp.bfloat16), "mp", axis=0, tiled=True)
    query_full, key_full, value_full, out_full, gate_full, up_full, down_full = (
        lax.all_gather(w_query, "dp", axis=0, tiled=True),
        lax.all_gather(w_key, "dp", axis=0, tiled=True),
        lax.all_gather(w_value, "dp", axis=0, tiled=True),
        lax.all_gather(w_out, "dp", axis=1, tiled=True),
        lax.all_gather(w_gate, "dp", axis=0, tiled=True),
        lax.all_gather(w_up, "dp", axis=0, tiled=True),
        lax.all_gather(w_down, "dp", axis=1, tiled=True),
    )
    gate = jnp.dot(hidden_rows, gate_full, preferred_element_type=jnp.float32)
    up_value = jnp.dot(hidden_rows, up_full, preferred_element_type=jnp.float32)
    sigma = jax.nn.sigmoid(gate)
    swish = gate * sigma
    act = (swish * up_value).astype(jnp.bfloat16)
    grad_act = times_transposed(grad_branch, down_full)
    grad_gate = (grad_act * up_value * sigma * (1.0 + gate * (1.0 - sigma))).astype(jnp.bfloat16)
    grad_up = (grad_act * swish).astype(jnp.bfloat16)
    grad_down_part = contract_rows(act, grad_branch)
    grad_gate_part = contract_rows(hidden_rows, grad_gate)
    grad_up_part = contract_rows(hidden_rows, grad_up)
    grad_gate_w, grad_up_w, grad_down_w = (
        lax.psum_scatter(grad_gate_part, "dp", scatter_dimension=0, tiled=True),
        lax.psum_scatter(grad_up_part, "dp", scatter_dimension=0, tiled=True),
        lax.psum_scatter(grad_down_part, "dp", scatter_dimension=1, tiled=True),
    )
    hidden_gradient = middle_gradient + lax.psum_scatter(
        (times_transposed(grad_gate, gate_full) + times_transposed(grad_up, up_full)).astype(
            jnp.bfloat16
        ),
        "mp",
        scatter_dimension=0,
        tiled=True,
    ).astype(jnp.float32)
    attention_gain_slice = jnp.sum(hidden_gradient * attention_normalized_input, axis=0)
    residual_gradient = layer_normalize_backward(
        hidden_gradient,
        attention_normalized_input,
        attention_inverse_deviation,
        attention_norm_gain,
    )
    grad_attn = lax.all_gather(residual_gradient.astype(jnp.bfloat16), "mp", axis=0, tiled=True)
    grad_context = times_transposed(grad_attn, out_full).astype(jnp.bfloat16)
    grad_out_part = contract_rows(context, grad_attn)
    query_grad, key_grad, value_grad = attention_backward(
        query, keys, values, split_heads(grad_context), row_seq, key_valid, logsum
    )
    grad_query = rotate_back(query_grad, cosine, sine).reshape(rows_grp, -1).astype(jnp.bfloat16)
    grad_key = rotate_back(key_grad, cosine, sine).reshape(rows_grp, -1).astype(jnp.bfloat16)
    grad_value = value_grad.reshape(rows_grp, -1).astype(jnp.bfloat16)
    grad_query_part = contract_rows(rows_all, grad_query)
    grad_key_part = contract_rows(rows_all, grad_key)
    grad_value_part = contract_rows(rows_all, grad_value)
    input_grad = (
        residual_gradient
        + lax.psum_scatter(
            (
                times_transposed(grad_query, query_full)
                + times_transposed(grad_key, key_full)
                + times_transposed(grad_value, value_full)
            ).astype(jnp.bfloat16),
            "mp",
            scatter_dimension=0,
            tiled=True,
        ).astype(jnp.float32)
    ).astype(jnp.bfloat16)
    grad_query_w, grad_key_w, grad_value_w, grad_out_w = (
        lax.psum_scatter(grad_query_part, "dp", scatter_dimension=0, tiled=True),
        lax.psum_scatter(grad_key_part, "dp", scatter_dimension=0, tiled=True),
        lax.psum_scatter(grad_value_part, "dp", scatter_dimension=0, tiled=True),
        lax.psum_scatter(grad_out_part, "dp", scatter_dimension=1, tiled=True),
    )
    grad_gain_attn, grad_gain_ffn = lax.psum(
        (attention_gain_slice, feedforward_gain_slice), ("dp", "mp")
    )
    return (
        output,
        input_grad,
        grad_query_w,
        grad_key_w,
        grad_value_w,
        grad_out_w,
        grad_gate_w,
        grad_up_w,
        grad_down_w,
        grad_gain_attn,
        grad_gain_ffn,
    )


def solution(mesh):
    return jax.shard_map(
        local,
        mesh=mesh,
        in_specs=(
            P(("dp", "mp"), None),
            P("dp", "mp"),
            P("dp", "mp"),
            P("dp", "mp"),
            P("mp", "dp"),
            P("dp", "mp"),
            P("dp", "mp"),
            P("mp", "dp"),
            P(),
            P(),
            P("dp", None),
            P("dp", None),
            P(("dp", "mp"), None),
        ),
        out_specs=(
            P(("dp", "mp"), None),
            P(("dp", "mp"), None),
            P("dp", "mp"),
            P("dp", "mp"),
            P("dp", "mp"),
            P("mp", "dp"),
            P("dp", "mp"),
            P("dp", "mp"),
            P("mp", "dp"),
            P(),
            P(),
        ),
        check_vma=False,
    )
```

profile of v0, /device:TPU:0, one launch (start us, length us, event | category | flops | bytes accessed | tf_op | source)
XLA Modules:
  0.0 2055.2 jit_solution(8183407351622684583)
XLA Ops:
  12.0 45.9 %all_gather.41 = bf16[768,384]{1,0:T(8,128)(2,1)S(1)} all-gather(bf16[48,384]{1,0:T(8,128)(2,1)} %param.18), channel_id=1, replica_groups=mesh['dp'=16,'mp'=2] {'dp'}, dimensions={0}, use_global_device_ids=true | all-gather | bytes 626688 | tf_op jit(solution)/shard_map/all_gather | solution.py:231
  57.9 39.2 %all_gather.42 = bf16[768,384]{1,0:T(8,128)(2,1)S(1)} all-gather(bf16[48,384]{1,0:T(8,128)(2,1)} %param.19), channel_id=1, replica_groups=mesh['dp'=16,'mp'=2] {'dp'}, dimensions={0}, use_global_device_ids=true | all-gather | bytes 626688 | tf_op jit(solution)/shard_map/all_gather | solution.py:232
  97.0 43.6 %all_gather.43 = bf16[768,384]{1,0:T(8,128)(2,1)} all-gather(bf16[48,384]{1,0:T(8,128)(2,1)} %param.20), channel_id=1, replica_groups=mesh['dp'=16,'mp'=2] {'dp'}, dimensions={0}, use_global_device_ids=true | all-gather | bytes 626688 | tf_op jit(solution)/shard_map/all_gather | solution.py:233
  140.6 41.5 %all_gather.44 = bf16[384,768]{0,1:T(8,128)(2,1)} all-gather(bf16[384,48]{0,1:T(8,128)(2,1)S(1)} %copy-done.26), channel_id=1, replica_groups=mesh['dp'=16,'mp'=2] {'dp'}, dimensions={1}, use_global_device_ids=true | all-gather | bytes 626688 | tf_op jit(solution)/shard_map/all_gather | solution.py:234
  192.9 147.9 %while.48 = (s32[]{:T(128)}, bf16[4,512,6,64]{1,3,2,0:T(8,128)(2,1)}, f32[4,6,512]{2,1,0:T(8,128)S(1)}, s32[4,512]{1,0:T(4,128)S(1)}, bf16[4,512,6,64]{1,3,2,0:T...) while((s32[]{:T(128)}, ...), condition=%wide.region_4.5_spmd.clone, body=%wide.region_1.4_spmd.clone.sunk | while | flops 1688415232 | bytes 83810680 | solution.py:121
  194.4 11.5 fusion.146
  206.0 12.0 fusion.147
  217.9 12.3 fusion.148
  231.3 11.5 fusion.146
  242.8 12.0 fusion.147
  254.8 12.3 fusion.148
  268.2 11.5 fusion.146
  279.7 12.0 fusion.147
  291.7 12.3 fusion.148
  305.0 11.5 fusion.146
  316.6 12.0 fusion.147
  328.6 12.3 fusion.148
  363.6 49.0 %all-gather.12.cloned.1.call-done = bf16[768,1536]{1,0:T(8,128)(2,1)} async-done(((bf16[48,1536]{1,0:T(8,128)(2,1)}), bf16[768,1536]{1,0:T(8,128)(2,1)}) %all-gather.12.cloned.1.call-update) | async-done | bytes 2359312 | tf_op jit(solution)/shard_map/all_gather | solution.py:264
  412.7 12.4 all-gather.10.cloned.1.call-done
  425.1 10.0 fusion.68
  435.0 56.9 %all-gather.14.cloned.1.call-done = bf16[768,1536]{1,0:T(8,128)(2,1)} async-done(((bf16[48,1536]{1,0:T(8,128)(2,1)}), bf16[768,1536]{1,0:T(8,128)(2,1)}) %all-gather.14.cloned.1.call-update) | async-done | bytes 2359312 | tf_op jit(solution)/shard_map/all_gather | solution.py:265
  491.9 14.1 multiply_convert_fusion.3
  506.0 49.9 %all-gather.16.cloned.1.call-done = bf16[1536,768]{0,1:T(8,128)(2,1)} async-done(((bf16[1536,48]{0,1:T(8,128)(2,1)}), bf16[1536,768]{0,1:T(8,128)(2,1)}) %all-gather.16.cloned.1.call-update) | async-done | bytes 2359312 | tf_op jit(solution)/shard_map/all_gather | solution.py:266
  555.9 9.1 convolution_convert_fusion.1
  565.0 9.3 reduce-scatter.20.cloned.1.call-done
  584.5 13.0 all-gather.18.cloned.1.call-done
  597.5 19.5 multiply_convert_fusion.1
  630.9 12.0 reduce-scatter.22.cloned.1.call-done
  650.6 13.4 all-gather.20.cloned.1.call-done
  676.0 399.6 %while.49 = (s32[]{:T(128)}, f32[2048,6,64]{0,2,1:T(8,128)}, f32[2048,6,64]{0,2,1:T(8,128)}, f32[4,512,6,64]{1,0,3,2:T(4,128)}, bf16[4,512,6,64]{1,3,2,0:T(8,128...) while((s32[]{:T(128)}, f32[2048,6,64]{0,2,1:T(8,128)}, ...), condition=%wide.region_18.19_spmd.clone, body=%wide.region_16.18_spmd.clone.sunk | while | flops 4127140864 | bytes 215906736 | solution.py:186
  677.3 11.1 fusion.158
  688.4 12.8 bitcast_add_fusion.5
  701.2 18.1 multiply_reduce_fusion.7
  719.3 21.3 %multiply_convert_fusion.7 = bf16[6,512,2048]{2,1,0:T(8,128)(2,1)} fusion(f32[6,512,2048]{2,1,0:T(8,128)} %get-tuple-element.560, f32[6,512,2048]{2,1,0:T(8,128)} %fusion.158, f32[6,512]{1,0:T(8,128)S(1)} %get-tuple-element.561, f32[6,512]{1,0:T(8,128)S(1)} %dynamic-slice_bitcast_fusion.2, pred[512,2048]{1,0:T(8,128)(4,1)S(1)} %compare_and_fusion.5), kind=kLoop, calls=%fused_computation.28.clone.1 | loop fusion | flops 37748736 | bytes 63987712 | tf_op jit(solution)/shard_map/while/body/eval_jaxpr/while/body/eval_jaxpr/convert_element_type | solution.py:163
  758.6 16.1 dynamic_update_slice.35
  775.7 11.1 fusion.158
  786.8 13.7 bitcast_add_fusion.5
  800.5 18.1 multiply_reduce_fusion.7
  818.6 21.3 %multiply_convert_fusion.7 = bf16[6,512,2048]{2,1,0:T(8,128)(2,1)} fusion(f32[6,512,2048]{2,1,0:T(8,128)} %get-tuple-element.560, f32[6,512,2048]{2,1,0:T(8,128)} %fusion.158, f32[6,512]{1,0:T(8,128)S(1)} %get-tuple-element.561, f32[6,512]{1,0:T(8,128)S(1)} %dynamic-slice_bitcast_fusion.2, pred[512,2048]{1,0:T(8,128)(4,1)S(1)} %compare_and_fusion.5), kind=kLoop, calls=%fused_computation.28.clone.1 | loop fusion | flops 37748736 | bytes 63987712 | tf_op jit(solution)/shard_map/while/body/eval_jaxpr/while/body/eval_jaxpr/convert_element_type | solution.py:163
  848.4 9.6 bitcast_add_fusion.4
  858.8 16.1 dynamic_update_slice.35
  875.9 11.1 fusion.158
  887.0 13.7 bitcast_add_fusion.5
  900.7 18.1 multiply_reduce_fusion.7
  918.8 21.3 %multiply_convert_fusion.7 = bf16[6,512,2048]{2,1,0:T(8,128)(2,1)} fusion(f32[6,512,2048]{2,1,0:T(8,128)} %get-tuple-element.560, f32[6,512,2048]{2,1,0:T(8,128)} %fusion.158, f32[6,512]{1,0:T(8,128)S(1)} %get-tuple-element.561, f32[6,512]{1,0:T(8,128)S(1)} %dynamic-slice_bitcast_fusion.2, pred[512,2048]{1,0:T(8,128)(4,1)S(1)} %compare_and_fusion.5), kind=kLoop, calls=%fused_computation.28.clone.1 | loop fusion | flops 37748736 | bytes 63987712 | tf_op jit(solution)/shard_map/while/body/eval_jaxpr/while/body/eval_jaxpr/convert_element_type | solution.py:163
  948.6 9.6 bitcast_add_fusion.4
  959.0 16.1 dynamic_update_slice.35
  976.1 11.1 fusion.158
  987.2 13.7 bitcast_add_fusion.5
  1000.9 18.1 multiply_reduce_fusion.7
  1019.0 21.3 %multiply_convert_fusion.7 = bf16[6,512,2048]{2,1,0:T(8,128)(2,1)} fusion(f32[6,512,2048]{2,1,0:T(8,128)} %get-tuple-element.560, f32[6,512,2048]{2,1,0:T(8,128)} %fusion.158, f32[6,512]{1,0:T(8,128)S(1)} %get-tuple-element.561, f32[6,512]{1,0:T(8,128)S(1)} %dynamic-slice_bitcast_fusion.2, pred[512,2048]{1,0:T(8,128)(4,1)S(1)} %compare_and_fusion.5), kind=kLoop, calls=%fused_computation.28.clone.1 | loop fusion | flops 37748736 | bytes 63987712 | tf_op jit(solution)/shard_map/while/body/eval_jaxpr/while/body/eval_jaxpr/convert_element_type | solution.py:163
  1048.8 9.6 bitcast_add_fusion.4
  1059.2 16.1 dynamic_update_slice.35
  1093.0 10.0 fusion.75
  1103.1 10.2 fusion.73
  1113.4 9.7 fusion.74
  1147.9 40.7 %all-reduce = (f32[768]{0:T(1024)}, f32[768]{0:T(1024)}) all-reduce(f32[768]{0:T(1024)S(1)} %copy-done.29, f32[768]{0:T(1024)S(1)} %copy-done.28), channel_id=1, replica_groups=mesh['dp'=16,'mp'=2] {'dp','mp'}, use_global_device_ids=true, to_apply=%region_28.29 | all-reduce | flops 1536 | bytes 12288 | tf_op jit(solution)/shard_map/psum | solution.py:362
  1191.5 57.6 %reduce-scatter.32.cloned.1.call-done = f32[1536,48]{0,1:T(8,128)} async-done(((f32[1536,768]{0,1:T(8,128)}), f32[1536,48]{0,1:T(8,128)}) %reduce-scatter.32.cloned.1.call-update) | async-done | bytes 294928 | tf_op jit(solution)/shard_map/reduce_scatter | solution.py:314
  1249.2 142.1 %reduce-scatter.28.cloned.1.call-done = f32[48,1536]{1,0:T(8,128)} async-done(((f32[768,1536]{1,0:T(8,128)}), f32[48,1536]{1,0:T(8,128)}) %reduce-scatter.28.cloned.1.call-update) | async-done | bytes 294928 | tf_op jit(solution)/shard_map/reduce_scatter | solution.py:312
  1391.2 141.9 %reduce-scatter.30.cloned.1.call-done = f32[48,1536]{1,0:T(8,128)} async-done(((f32[768,1536]{1,0:T(8,128)}), f32[48,1536]{1,0:T(8,128)}) %reduce-scatter.30.cloned.1.call-update) | async-done | bytes 294928 | tf_op jit(solution)/shard_map/reduce_scatter | solution.py:313
  1533.1 128.7 %reduce-scatter.26.cloned.1.call-done = f32[384,48]{0,1:T(8,128)} async-done(((f32[384,768]{0,1:T(8,128)}), f32[384,48]{0,1:T(8,128)}) %reduce-scatter.26.cloned.1.call-update) | async-done | bytes 73744 | tf_op jit(solution)/shard_map/reduce_scatter | solution.py:360
  1661.8 128.7 %reduce-scatter.36.cloned.1.call-done = f32[48,384]{1,0:T(8,128)} async-done(((f32[768,384]{1,0:T(8,128)}), f32[48,384]{1,0:T(8,128)}) %reduce-scatter.36.cloned.1.call-update) | async-done | bytes 73744
  1790.5 128.5 %reduce-scatter.34.cloned.1.call-done = f32[48,384]{1,0:T(8,128)} async-done(((f32[768,384]{1,0:T(8,128)}), f32[48,384]{1,0:T(8,128)}) %reduce-scatter.34.cloned.1.call-update) | async-done | bytes 73744
  1919.0 128.7 %reduce-scatter.38.cloned.1.call-done = f32[48,384]{1,0:T(8,128)} async-done(((f32[768,384]{1,0:T(8,128)}), f32[48,384]{1,0:T(8,128)}) %reduce-scatter.38.cloned.1.call-update) | async-done | bytes 73744
  (245 shorter events, 180.2 us)
Async XLA Ops:
  8.0 132.6 %copy-start.26 = (bf16[384,48]{0,1:T(8,128)(2,1)S(1)}, bf16[384,48]{0,1:T(8,128)(2,1)}, u32[]{:S(2)}) copy-start(bf16[384,48]{0,1:T(8,128)(2,1)} %param.21) | copy-start | bytes 110596
  8.0 175.1 %all-gather.8.cloned.1.call-start = ((), (), s32[]{:S(2)}) async-start(), calls=%async_computation.11 | async-start | bytes 4718592 | tf_op jit(solution)/shard_map/all_gather | solution.py:229
  8.8 348.8 %reduce-scatter.18.cloned.1.call-start = ((), (), s32[]{:S(2)}) async-start(), calls=%async_computation.12 | async-start | bytes 4718592 | tf_op jit(solution)/shard_map/reduce_scatter | solution.py:252
  57.9 128.8 %copy-start.15 = (bf16[768,384]{1,0:T(8,128)(2,1)}, bf16[768,384]{1,0:T(8,128)(2,1)S(1)}, u32[]{:S(2)}) copy-start(bf16[768,384]{1,0:T(8,128)(2,1)S(1)} %all_gather.41) | copy-start | bytes 1769476
  97.0 89.7 %copy-start.13 = (bf16[768,384]{1,0:T(8,128)(2,1)}, bf16[768,384]{1,0:T(8,128)(2,1)S(1)}, u32[]{:S(2)}) copy-start(bf16[768,384]{1,0:T(8,128)(2,1)S(1)} %all_gather.42) | copy-start | bytes 1769476
  183.1 5.1 copy-start.17
  183.1 5.1 copy-start.19
  183.1 3.6 copy-start.30
  189.3 2.1 copy-start.11
  191.4 1.5 copy-start.24
  191.4 1.5 copy-start.25
  340.8 3.7 copy-start.4
  340.9 4.9 copy-start.22
  344.5 1.2 copy-start.21
  349.2 8.3 copy-start.1
  349.2 63.5 %all-gather.12.cloned.1.call-start = ((), (), s32[]{:S(2)}) async-start(), calls=%async_computation.14 | async-start | bytes 2506752 | tf_op jit(solution)/shard_map/all_gather | solution.py:264
  349.8 10.6 copy-start.23
  349.8 75.2 %all-gather.10.cloned.1.call-start = ((), (), s32[]{:S(2)}) async-start(), calls=%async_computation.13 | async-start | bytes 4718592 | tf_op jit(solution)/shard_map/all_gather | solution.py:268
  357.5 2.1 copy-start.2
  362.3 129.6 %all-gather.14.cloned.1.call-start = ((), (), s32[]{:S(2)}) async-start(), calls=%async_computation.15 | async-start | bytes 2506752 | tf_op jit(solution)/shard_map/all_gather | solution.py:265
  362.9 193.0 %all-gather.16.cloned.1.call-start = ((), (), s32[]{:S(2)}) async-start(), calls=%async_computation.16 | async-start | bytes 2506752 | tf_op jit(solution)/shard_map/all_gather | solution.py:266
  363.6 210.7 %reduce-scatter.20.cloned.1.call-start = ((), (), s32[]{:S(2)}) async-start(), calls=%async_computation.17 | async-start | bytes 4718592 | tf_op jit(solution)/shard_map/reduce_scatter | solution.py:272
  565.0 32.5 %all-gather.18.cloned.1.call-start = ((), (), s32[]{:S(2)}) async-start(), calls=%async_computation.18 | async-start | bytes 4718592 | tf_op jit(solution)/shard_map/all_gather | solution.py:290
  577.4 1.4 copy-start.7
  577.4 1.4 copy-start.27
  584.1 58.8 %reduce-scatter.22.cloned.1.call-start = ((), (), s32[]{:S(2)}) async-start(), calls=%async_computation.19 | async-start | bytes 4718592 | tf_op jit(solution)/shard_map/reduce_scatter | solution.py:316
  597.5 19.5 copy-start.31
  617.0 7.3 copy-start.32
  617.0 7.4 copy-start.33
  630.8 33.2 %all-gather.20.cloned.1.call-start = ((), (), s32[]{:S(2)}) async-start(), calls=%async_computation.20 | async-start | bytes 4718592 | tf_op jit(solution)/shard_map/all_gather | solution.py:331
  642.9 4.5 copy-start.3
  642.9 4.5 copy-start.5
  642.9 4.7 copy-start.10
  650.5 538.1 %reduce-scatter.24.cloned.1.call-start = ((), (), s32[]{:S(2)}) async-start(), calls=%async_computation.21 | async-start | bytes 4718592 | tf_op jit(solution)/shard_map/reduce_scatter | solution.py:345
  1079.5 2.8 copy-start
  1079.6 2.8 copy-start.18
  1079.6 2.9 copy-start.20
  1081.8 7.4 copy-start.8
  1083.5 1.1 copy-start.16
  1086.4 1.1 copy-start.14
  1087.4 1.9 copy-start.12
  1092.9 156.2 %reduce-scatter.32.cloned.1.call-start = ((), (), s32[]{:S(2)}) async-start(), calls=%async_computation.25 | async-start | bytes 5013504 | tf_op jit(solution)/shard_map/reduce_scatter | solution.py:314
  1103.0 288.2 %reduce-scatter.28.cloned.1.call-start = ((), (), s32[]{:S(2)}) async-start(), calls=%async_computation.23 | async-start | bytes 5013504 | tf_op jit(solution)/shard_map/reduce_scatter | solution.py:312
  1113.3 419.8 %reduce-scatter.30.cloned.1.call-start = ((), (), s32[]{:S(2)}) async-start(), calls=%async_computation.24 | async-start | bytes 5013504 | tf_op jit(solution)/shard_map/reduce_scatter | solution.py:313
  1123.1 538.7 %reduce-scatter.26.cloned.1.call-start = ((), (), s32[]{:S(2)}) async-start(), calls=%async_computation.22 | async-start | bytes 1253376 | tf_op jit(solution)/shard_map/reduce_scatter | solution.py:360
  1128.6 661.9 %reduce-scatter.36.cloned.1.call-start = ((), (), s32[]{:S(2)}) async-start(), calls=%async_computation.27 | async-start | bytes 1253376
  1135.7 783.3 %reduce-scatter.34.cloned.1.call-start = ((), (), s32[]{:S(2)}) async-start(), calls=%async_computation.26 | async-start | bytes 1253376
  1139.0 1.7 copy-start.9
  1140.5 907.2 %reduce-scatter.38.cloned.1.call-start = ((), (), s32[]{:S(2)}) async-start(), calls=%async_computation.28 | async-start | bytes 1253376
  1145.0 2.9 copy-start.28
  1145.0 2.9 copy-start.29
  1145.0 43.6 %copy-start.6 = (f32[1024,768]{1,0:T(8,128)S(1)}, f32[1024,768]{1,0:T(8,128)}, u32[]{:S(2)}) copy-start(f32[1024,768]{1,0:T(8,128)} %get-tuple-element.396) | copy-start | bytes 9437188
Sparse Core Ops, SparseCore 0:
  10.4 14.8 all-gather.7
  349.3 8.1 reduce-scatter.17
  565.1 9.1 reduce-scatter.19
  584.2 13.2 all-gather.17
  650.7 13.3 all-gather.19
  1093.1 12.0 reduce-scatter.23
  1110.9 138.2 reduce-scatter.31
  1255.7 135.4 reduce-scatter.27
  1397.0 136.0 reduce-scatter.29
  1539.0 122.7 reduce-scatter.25
  1667.8 122.5 reduce-scatter.35
  1796.4 122.5 reduce-scatter.33
  1925.0 122.6 reduce-scatter.37
Sparse Core Ops, SparseCore 1:
  352.9 59.7 all-gather.11
  414.7 10.2 all-gather.9
  428.1 63.7 all-gather.13
  495.1 60.8 all-gather.15
  630.9 11.9 reduce-scatter.21
where the time goes:
time: 2060 us
  waiting for transfers between devices  1080 us (52%)
  matrix products  473 us (23%)
  blocking collectives  211 us (10%)
  other arithmetic  171 us (8%)
  local copies, waits for them, and re-layouts  99.2 us (5%)
    unnamed x21, waiting for transfers between devices  389 us
    reduce_scatter x1, waiting for transfers between devices, local(): lax.psum_scatter(grad_gate_part, 'dp', scatter_dimension=0, tiled=True)  142 us
    reduce_scatter x1, waiting for transfers between devices, local(): lax.psum_scatter(grad_up_part, 'dp', scatter_dimension=0, tiled=True)  142 us
    reduce_scatter x1, waiting for transfers between devices, local(): lax.psum_scatter(grad_out_part, 'dp', scatter_dimension=1, tiled=True)  129 us
    dot_general x8, matrix products, one_block(): jnp.einsum('qhd,khd->hqk', query_block, key_pack, preferred_element_type=...  90.6 us
    convert_element_type x4, other arithmetic, one_block(): grad_scores = (probs * (grad_probs - delta)).astype(jnp.bfloat16)  85 us
    dot_general x4, matrix products, one_block(): jnp.einsum('qhd,khd->hqk', grad_block, value_pack, preferred_element_type...  72.5 us
    dynamic_update_slice x8, local copies, waits for them, and re-layouts, one_pack(): lax.scan(one_block, (zeros, zeros), (query_pack, grad_pack, seq_pack.resh...  67.5 us
  transfers between devices with their start and end apart: 18, of which 16 were waited for; matrix products, arithmetic and copies ran while one was open for 4% of the time, Pallas kernels for 0%

commit v1 on v0

v1 whole, which is shorter than its diff:
```python
import functools
import math

import jax
import jax.numpy as jnp
from jax import lax
from jax.experimental import pallas as pl
from jax.experimental.pallas import tpu as pltpu
from jax.sharding import Mesh
from jax.sharding import PartitionSpec as P

HEAD_DIM = 64
SEQ_MAX = 2048
QLEN = 64
EPS = 1e-05
ROPE_BASE = 1000.0
MASKED = -1e30
SLOT = 128

bf16 = jnp.bfloat16
f32 = jnp.float32

NN = (((1,), (0,)), ((), ()))
NT = (((1,), (1,)), ((), ()))


def dot(left, right, dims=NN):
    return lax.dot_general(left, right, dims, preferred_element_type=f32)


def call(kernel, name, grid, in_specs, out_specs, out_shape, flops, scratch=(), aliases=None, exps=0):
    def run(*operands):
        outs = out_shape if isinstance(out_shape, (list, tuple)) else [out_shape]
        moved = sum(math.prod(o.shape) * o.dtype.itemsize for o in (*operands, *outs))
        return pl.pallas_call(
            kernel,
            name=name,
            grid=grid,
            in_specs=in_specs,
            out_specs=out_specs,
            out_shape=out_shape,
            scratch_shapes=list(scratch),
            input_output_aliases=aliases or {},
            cost_estimate=pl.CostEstimate(
                flops=int(flops), bytes_accessed=int(moved), transcendentals=int(exps)
            ),
            compiler_params=pltpu.CompilerParams(vmem_limit_bytes=60 * 1024 * 1024),
        )(*operands)

    return run


def shape(dims, dtype):
    return jax.ShapeDtypeStruct(dims, dtype)


def whole(dims):
    return pl.BlockSpec(dims, lambda *_: (0,) * len(dims))


def rope(value, cosine, sine, lane):
    half = HEAD_DIM // 2
    lanes = value.shape[-1]
    swapped = jnp.where(
        lane % HEAD_DIM < half,
        pltpu.roll(value, lanes - half, 1),
        pltpu.roll(value, half, 1),
    )
    return value * cosine + swapped * sine


def qkv_kernel(own_blocks, own_ref, par_ref, w_ref, cos_ref, sin_ref, eq_ref, ek_ref, q_ref, k_ref, v_ref):
    rows = jnp.where(pl.program_id(0) < own_blocks, own_ref[...], par_ref[...])
    lane = lax.broadcasted_iota(jnp.int32, (rows.shape[0], SLOT), 1)
    low = lane < HEAD_DIM
    ones = jnp.where((lane >= HEAD_DIM) & (lane < HEAD_DIM + 3), -1.0, 0.0)
    cosine, sine = cos_ref[...], sin_ref[...]
    ext_q, ext_k = eq_ref[...].astype(f32), ek_ref[...].astype(f32)
    for pair in range(q_ref.shape[0] // 2):
        base = pair * 3 * SLOT
        mixed = dot(rows, w_ref[:, base : base + 3 * SLOT])
        query = rope(mixed[:, :SLOT], cosine, sine, lane) * HEAD_DIM**-0.5
        key = rope(mixed[:, SLOT : 2 * SLOT], cosine, sine, lane)
        value = mixed[:, 2 * SLOT :]
        for ref, data, ext in ((q_ref, query, ext_q), (k_ref, key, ext_k), (v_ref, value, ones)):
            ref[2 * pair] = jnp.where(low, data, ext).astype(bf16)
            ref[2 * pair + 1] = jnp.where(low, pltpu.roll(data, HEAD_DIM, 1), ext).astype(bf16)


def project_qkv(own, par, weights, cosine, sine, ext_q, ext_k, block=256):
    rows, width = own.shape
    heads = weights.shape[1] // (3 * HEAD_DIM)
    count = rows // block
    table = pl.BlockSpec((block, SLOT), lambda i: (i, 0))
    out = pl.BlockSpec((heads, block, SLOT), lambda i: (0, i, 0))
    return call(
        functools.partial(qkv_kernel, count),
        "project_qkv",
        (2 * count,),
        [
            pl.BlockSpec((block, width), lambda i: (jnp.minimum(i, count - 1), 0)),
            pl.BlockSpec((block, width), lambda i: (jnp.maximum(i - count, 0), 0)),
            whole(weights.shape),
            table,
            table,
            table,
            table,
        ],
        [out] * 3,
        [shape((heads, 2 * rows, SLOT), bf16)] * 3,
        4 * rows * width * weights.shape[1],
    )(own, par, weights, cosine, sine, ext_q, ext_k)


def split_three(value):
    first = value.astype(bf16).astype(f32)
    second = (value - first).astype(bf16).astype(f32)
    return first, second, value - first - second


def attend_kernel(block, q_ref, k_ref, v_ref, ctx_ref, mix_ref, q2_ref):
    lane = lax.broadcasted_iota(jnp.int32, (block, SLOT), 1)
    low = lane < HEAD_DIM
    for piece in range(q_ref.shape[1] // block):
        rows = pl.ds(piece * block, block)
        mixed = []
        for head in range(2):
            query = q_ref[head, rows, :]
            scores = dot(query, k_ref[head], NT)
            peak = jnp.max(scores, axis=-1, keepdims=True)
            expo = jnp.exp(scores - peak).astype(bf16)
            total_mix = dot(expo, v_ref[head])
            total = -total_mix[:, HEAD_DIM : HEAD_DIM + 1]
            mixed.append(total_mix * (1.0 / total))
            parts = split_three(peak + jnp.log(total))
            kept = query.astype(f32)
            for at, part in enumerate(parts):
                kept = jnp.where(lane == HEAD_DIM + 32 + at, part, kept)
            q2_ref[head, rows, :] = kept.astype(bf16)
        both = jnp.where(low, mixed[0], pltpu.roll(mixed[1], HEAD_DIM, 1))
        mix_ref[rows, :] = both
        ctx_ref[rows, :] = both.astype(bf16)


def attend(query, keys, values, block=256, step=512):
    heads, rows, _ = query.shape
    piece = pl.BlockSpec((2, step, SLOT), lambda p, i: (p, i, 0))
    full = pl.BlockSpec((2, rows, SLOT), lambda p, i: (p, 0, 0))
    out = pl.BlockSpec((step, SLOT), lambda p, i: (i, p))
    width = heads * HEAD_DIM
    return call(
        functools.partial(attend_kernel, block),
        "attend",
        (heads // 2, rows // step),
        [piece, full, full],
        [out, out, piece],
        [shape((rows, width), bf16), shape((rows, width), f32), shape(query.shape, bf16)],
        4 * heads * rows * rows * SLOT,
        exps=heads * rows * rows,
    )(query, keys, values)


def attend_back_kernel(
    block, q_ref, k_ref, v_ref, own_ref, par_ref, mix_ref, cos_ref, sin_ref, out_ref, g_ref, acc_ref
):
    at = pl.program_id(0)
    rows = q_ref.shape[1]
    half = own_ref.shape[0]
    lane = lax.broadcasted_iota(jnp.int32, (half, SLOT), 1)
    low = lane < HEAD_DIM

    @pl.when(at == 0)
    def _():
        acc_ref[...] = jnp.zeros_like(acc_ref)
        for part, grad_ref in enumerate((own_ref, par_ref)):
            span = pl.ds(part * half, half)
            grad = grad_ref[...].astype(f32)
            product = grad * mix_ref[span, :]
            for head in range(2):
                mine = low if head == 0 else ~low
                delta = jnp.sum(jnp.where(mine, product, 0.0), axis=-1, keepdims=True)
                kept = grad if head == 0 else pltpu.roll(grad, HEAD_DIM, 1)
                kept = jnp.where(low, kept, 0.0)
                for n, piece in enumerate(split_three(delta)):
                    kept = jnp.where(lane == HEAD_DIM + n, piece, kept)
                g_ref[head, span, :] = kept.astype(bf16)

    step = k_ref.shape[1]
    lane_k = lax.broadcasted_iota(jnp.int32, (block, SLOT), 1)
    low_k = lane_k < HEAD_DIM
    for piece in range(step // block):
        span = pl.ds(piece * block, block)
        grads = []
        for head in range(2):
            keys, values = k_ref[head, span, :], v_ref[head, span, :]
            probs = jnp.exp(dot(keys, q_ref[head], NT))
            grad_scores = (probs * dot(values, g_ref[head], NT)).astype(bf16)
            grad_value = dot(probs.astype(bf16), g_ref[head])
            grad_key = dot(grad_scores, q_ref[head])
            acc_ref[head] += lax.dot_general(
                keys, grad_scores, (((0,), (0,)), ((), ())), preferred_element_type=f32
            )
            grads.append((grad_key, grad_value))
        grad_key, grad_value = (
            jnp.where(low_k, first, pltpu.roll(second, HEAD_DIM, 1))
            for first, second in zip(*grads)
        )
        place = pl.ds(pl.multiple_of(at * step + piece * block, block), block)
        grad_key = rope(grad_key, cos_ref[place, :], -sin_ref[place, :], lane_k)
        out_ref[place, SLOT : 2 * SLOT] = grad_key.astype(bf16)
        out_ref[place, 2 * SLOT :] = grad_value.astype(bf16)

    @pl.when(at == pl.num_programs(0) - 1)
    def _():
        grad_query = jnp.where(
            lax.broadcasted_iota(jnp.int32, (rows, SLOT), 1) < HEAD_DIM,
            acc_ref[0].T,
            pltpu.roll(acc_ref[1].T, HEAD_DIM, 1),
        )
        turned = rope(
            grad_query,
            cos_ref[...],
            -sin_ref[...],
            lax.broadcasted_iota(jnp.int32, (rows, SLOT), 1),
        )
        out_ref[:, :SLOT] = (turned * HEAD_DIM**-0.5).astype(bf16)


def attend_back(pair, query, keys, values, own, par, mixed, cosine, sine, block=256, step=512):
    heads, rows, _ = query.shape
    half = own.shape[0]
    full = pl.BlockSpec((2, rows, SLOT), lambda i: (pair, 0, 0))
    piece = pl.BlockSpec((2, step, SLOT), lambda i: (pair, i, 0))
    grad = pl.BlockSpec((half, SLOT), lambda i: (0, pair))
    return call(
        functools.partial(attend_back_kernel, block),
        "attend_back",
        (rows // step,),
        [
            full,
            piece,
            piece,
            grad,
            grad,
            pl.BlockSpec((rows, SLOT), lambda i: (0, pair)),
            whole((rows, SLOT)),
            whole((rows, SLOT)),
        ],
        whole((rows, 3 * SLOT)),
        shape((rows, 3 * SLOT), bf16),
        10 * 2 * rows * rows * SLOT,
        scratch=[pltpu.VMEM((2, rows, SLOT), bf16), pltpu.VMEM((2, SLOT, rows), f32)],
        exps=2 * rows * rows,
    )(query, keys, values, own, par, mixed, cosine, sine)


def normalize(value):
    mean = jnp.mean(value, axis=-1, keepdims=True)
    centred = value - mean
    inverse = lax.rsqrt(jnp.mean(centred * centred, axis=-1, keepdims=True) + EPS)
    return centred * inverse, inverse


def normalize_back(grad, xhat, inverse, gain):
    scaled = grad * gain
    return inverse * (
        scaled
        - jnp.mean(scaled, axis=-1, keepdims=True)
        - xhat * jnp.mean(scaled * xhat, axis=-1, keepdims=True)
    )


def fold_rows(value):
    return jnp.sum(value.reshape(-1, 8, value.shape[-1]), axis=0)


def attention_out_kernel(ctx_ref, got_ref, mine_ref, other_ref, tok_ref, gain_ref, xhat_ref, inv_ref, low_ref):
    branch = dot(ctx_ref[...], mine_ref[...], NT) + dot(got_ref[...], other_ref[...], NT)
    xhat, inverse = normalize(tok_ref[...].astype(f32) + branch)
    xhat_ref[...] = xhat
    inv_ref[...] = inverse
    low_ref[...] = (xhat * gain_ref[...]).astype(bf16)


def attention_out(ctx, got, mine, other, at, tokens, gain, block=256):
    rows, width = tokens.shape
    half = got.shape[1]
    piece = pl.BlockSpec((block, half), lambda i: (i, 0))
    row = pl.BlockSpec((block, width), lambda i: (i, 0))
    return call(
        attention_out_kernel,
        "attention_out",
        (rows // block,),
        [
            piece,
            piece,
            pl.BlockSpec((width, half), lambda i: (0, at // half)),
            whole(other.shape),
            row,
            whole((1, width)),
        ],
        [row, pl.BlockSpec((block, 1), lambda i: (i, 0)), row],
        [shape((rows, width), f32), shape((rows, 1), f32), shape((rows, width), bf16)],
        4 * rows * width * half,
    )(ctx, got, mine, other, tokens, gain)


def gate_up_kernel(block, x_ref, gate_ref, up_ref, act_ref, da_ref, db_ref):
    for piece in range(x_ref.shape[0] // block):
        span = pl.ds(piece * block, block)
        gate = dot(x_ref[span, :], gate_ref[...])
        up = dot(x_ref[span, :], up_ref[...])
        sigma = jax.nn.sigmoid(gate)
        swish = gate * sigma
        act_ref[span, :] = (swish * up).astype(bf16)
        da_ref[span, :] = (up * (sigma * (1.0 + gate * (1.0 - sigma)))).astype(bf16)
        db_ref[span, :] = swish.astype(bf16)


def gate_up(x, weights, units, tile=256, block=256):
    rows, width = x.shape
    count = units // tile
    out = pl.BlockSpec((rows, tile), lambda n: (0, n))
    return call(
        functools.partial(gate_up_kernel, block),
        "gate_up",
        (count,),
        [
            whole((rows, width)),
            pl.BlockSpec((width, tile), lambda n: (0, n)),
            pl.BlockSpec((width, tile), lambda n: (0, count + n)),
        ],
        [out] * 3,
        [shape((rows, units), bf16)] * 3,
        4 * rows * width * units,
    )(x, weights, weights)


def down_kernel(act_ref, down_ref, out_ref):
    out_ref[...] = dot(act_ref[...], down_ref[...], NT).astype(bf16)


def down(act, weights, at, block=256):
    rows, units = act.shape
    width = weights.shape[0]
    return call(
        down_kernel,
        "down",
        (rows // block,),
        [
            pl.BlockSpec((block, units), lambda i: (i, 0)),
            pl.BlockSpec((width, units), lambda i: (0, at // units)),
        ],
        pl.BlockSpec((block, width), lambda i: (i, 0)),
        shape((rows, width), bf16),
        2 * rows * width * units,
    )(act, weights)


def down_norm_kernel(
    act_ref, down_ref, got_ref, xhat_ref, cot_ref, gain_a_ref, gain_f_ref, out_ref, mid_ref, low_ref, sum_ref
):
    branch = dot(act_ref[...], down_ref[...], NT) + got_ref[...].astype(f32)
    xhat, inverse = normalize(xhat_ref[...] * gain_a_ref[...] + branch)
    gain = gain_f_ref[...]
    out_ref[...] = (xhat * gain).astype(bf16)
    grad = cot_ref[...].astype(f32)
    middle = normalize_back(grad, xhat, inverse, gain)
    mid_ref[...] = middle
    low_ref[...] = middle.astype(bf16)

    @pl.when(pl.program_id(0) == 0)
    def _():
        sum_ref[...] = jnp.zeros_like(sum_ref)

    sum_ref[...] += fold_rows(grad * xhat)


def down_norm(act, weights, at, got, xhat, cotangent, gain_a, gain_f, block=256):
    rows, units = act.shape
    width = weights.shape[0]
    row = pl.BlockSpec((block, width), lambda i: (i, 0))
    return call(
        down_norm_kernel,
        "down_norm",
        (rows // block,),
        [
            pl.BlockSpec((block, units), lambda i: (i, 0)),
            pl.BlockSpec((width, units), lambda i: (0, at // units)),
            row,
            row,
            row,
            whole((1, width)),
            whole((1, width)),
        ],
        [row, row, row, whole((8, width))],
        [
            shape((rows, width), bf16),
            shape((rows, width), f32),
            shape((rows, width), bf16),
            shape((8, width), f32),
        ],
        2 * rows * width * units,
    )(act, weights, got, xhat, cotangent, gain_a, gain_f)


def gate_up_back_kernel(block, g_ref, down_ref, da_ref, db_ref, gate_ref, up_ref):
    for piece in range(g_ref.shape[0] // block):
        span = pl.ds(piece * block, block)
        grad = dot(g_ref[span, :], down_ref[...])
        gate_ref[span, :] = (grad * da_ref[span, :].astype(f32)).astype(bf16)
        up_ref[span, :] = (grad * db_ref[span, :].astype(f32)).astype(bf16)


def gate_up_back(grad, weights, at, da, db, tile=256, block=256):
    rows, width = grad.shape
    units = da.shape[1]
    out = pl.BlockSpec((rows, tile), lambda n: (0, n))
    return call(
        functools.partial(gate_up_back_kernel, block),
        "gate_up_back",
        (units // tile,),
        [
            whole((rows, width)),
            pl.BlockSpec((width, tile), lambda n: (0, at // tile + n)),
            out,
            out,
        ],
        [out, out],
        [shape((rows, units), bf16)] * 2,
        2 * rows * width * units,
    )(grad, weights, da, db)


def hidden_back_kernel(gate_ref, up_ref, wg_ref, wu_ref, out_ref):
    out_ref[...] = (
        dot(gate_ref[...], wg_ref[...], NT) + dot(up_ref[...], wu_ref[...], NT)
    ).astype(bf16)


def hidden_back(gate, up, weights, block=256):
    rows, units = gate.shape
    width = weights.shape[0]
    piece = pl.BlockSpec((block, units), lambda i: (i, 0))
    return call(
        hidden_back_kernel,
        "hidden_back",
        (rows // block,),
        [
            piece,
            piece,
            pl.BlockSpec((width, units), lambda i: (0, 0)),
            pl.BlockSpec((width, units), lambda i: (0, 1)),
        ],
        pl.BlockSpec((block, width), lambda i: (i, 0)),
        shape((rows, width), bf16),
        4 * rows * width * units,
    )(gate, up, weights, weights)


def hidden_norm_back_kernel(
    gate_ref,
    up_ref,
    wg_ref,
    wu_ref,
    got_ref,
    mid_ref,
    xhat_ref,
    inv_ref,
    gain_ref,
    mine_ref,
    other_ref,
    res_ref,
    low_ref,
    keep_ref,
    send_ref,
    sum_ref,
):
    grad = (
        mid_ref[...]
        + got_ref[...].astype(f32)
        + dot(gate_ref[...], wg_ref[...], NT)
        + dot(up_ref[...], wu_ref[...], NT)
    )
    xhat = xhat_ref[...]
    residual = normalize_back(grad, xhat, inv_ref[...], gain_ref[...])
    res_ref[...] = residual
    low = residual.astype(bf16)
    low_ref[...] = low
    keep_ref[...] = dot(low, mine_ref[...]).astype(bf16)
    send_ref[...] = dot(low, other_ref[...]).astype(bf16)

    @pl.when(pl.program_id(0) == 0)
    def _():
        sum_ref[...] = jnp.zeros_like(sum_ref)

    sum_ref[...] += fold_rows(grad * xhat)


def hidden_norm_back(gate, up, weights, got, middle, xhat, inverse, gain, at, other, block=256):
    rows, units = gate.shape
    width, half = other.shape
    piece = pl.BlockSpec((block, units), lambda i: (i, 0))
    row = pl.BlockSpec((block, width), lambda i: (i, 0))
    part = pl.BlockSpec((block, half), lambda i: (i, 0))
    return call(
        hidden_norm_back_kernel,
        "hidden_norm_back",
        (rows // block,),
        [
            piece,
            piece,
            pl.BlockSpec((width, units), lambda i: (0, 0)),
            pl.BlockSpec((width, units), lambda i: (0, 1)),
            row,
            row,
            row,
            pl.BlockSpec((block, 1), lambda i: (i, 0)),
            whole((1, width)),
            pl.BlockSpec((width, half), lambda i: (0, at // half)),
            whole(other.shape),
        ],
        [row, row, part, part, whole((8, width))],
        [
            shape((rows, width), f32),
            shape((rows, width), bf16),
            shape((rows, half), bf16),
            shape((rows, half), bf16),
            shape((8, width), f32),
        ],
        4 * rows * width * (units + half),
    )(gate, up, weights, weights, got, middle, xhat, inverse, gain, weights, other)


def weight_grad_kernel(outer, inner, own_ref, par_ref, yo_ref, yp_ref, *refs):
    out_ref, turned_ref = refs[-2:]
    rows, width = own_ref.shape

    @pl.when(pl.program_id(0) == 0)
    def _():
        turned_ref[:, :rows] = own_ref[...].T
        turned_ref[:, rows:] = par_ref[...].T

    total = dot(turned_ref[:, :rows], yo_ref[...]) + dot(turned_ref[:, rows:], yp_ref[...])
    total = total.astype(bf16)
    if outer is None:
        out_ref[...] = total
    else:
        depth = width // (outer * inner)
        for hi in range(outer):
            for lo in range(inner):
                start = (hi * inner + lo) * depth
                out_ref[lo, hi] = total[start : start + depth]


def weight_grad(split, own, par, grad_own, grad_par, halves, columns, at, tile, into=None):
    rows, width = own.shape
    n = grad_own.shape[1]
    first = at // tile
    outer, inner = split if split else (None, None)
    if split:
        dims = (inner, outer, width // (outer * inner), columns)
        out = pl.BlockSpec((*dims[:3], tile), lambda i: (0, 0, 0, first + i))
    else:
        dims = (width, columns)
        out = pl.BlockSpec((width, tile), lambda i: (0, first + i))
    lower = halves
    operands = [own, par, grad_own, grad_par]
    specs = [
        whole((rows, width)),
        whole((rows, width)),
        pl.BlockSpec((rows, tile), lambda i: (0, i)),
        pl.BlockSpec((rows, tile), lambda i: (lower, i)),
    ]
    aliases = None
    if into is not None:
        operands.append(into)
        specs.append(pl.BlockSpec(memory_space=pl.ANY))
        aliases = {4: 0}
    return call(
        functools.partial(weight_grad_kernel, outer, inner),
        "weight_grad",
        (n // tile,),
        specs,
        out,
        shape(dims, bf16),
        4 * rows * width * n,
        scratch=[pltpu.VMEM((width, 2 * rows), bf16)],
        aliases=aliases,
    )(*operands)


def input_back_kernel(*refs):
    *piece_refs, w_ref, out_ref = refs
    joined = jnp.concatenate([ref[...] for ref in piece_refs], axis=1)
    out_ref[...] = dot(joined, w_ref[...], NT).astype(bf16)


def input_back_add_kernel(*refs):
    *piece_refs, w_ref, res_ref, got_ref, out_ref = refs
    joined = jnp.concatenate([ref[...] for ref in piece_refs], axis=1)
    total = dot(joined, w_ref[...], NT) + res_ref[...] + got_ref[...].astype(f32)
    out_ref[...] = total.astype(bf16)


def input_back(pieces, weights, lower, extra=(), block=256):
    rows = pieces[0].shape[0] // 2
    width, columns = weights.shape
    count = rows // block
    first = count if lower else 0
    row = pl.BlockSpec((block, width), lambda i: (i, 0))
    return call(
        input_back_add_kernel if extra else input_back_kernel,
        "input_back",
        (count,),
        [pl.BlockSpec((block, p.shape[1]), lambda i: (first + i, 0)) for p in pieces]
        + [whole(weights.shape)]
        + [row] * len(extra),
        row,
        shape((rows, width), bf16),
        2 * rows * width * columns,
    )(*pieces, weights, *extra)


def swap(value):
    return lax.ppermute(value, "mp", [(0, 1), (1, 0)])


def sum_everywhere(value, axes):
    for axis, size in axes:
        if size & (size - 1):
            return lax.psum(value, tuple(name for name, _ in axes))
    for axis, size in axes:
        step = 1
        while step < size:
            value = value + lax.ppermute(value, axis, [(i, i ^ step) for i in range(size)])
            step *= 2
    return value


def gather_rows(shard, split):
    if not split:
        return lax.all_gather(shard, ("hi", "lo"), axis=0, tiled=True)
    return lax.all_gather(shard, ("hi", "lo"), axis=0, tiled=True)


def scatter_rows(partial, split):
    if not split:
        return lax.psum_scatter(partial, ("hi", "lo"), scatter_dimension=0, tiled=True)
    once = lax.psum_scatter(partial, "lo", scatter_dimension=0, tiled=False)
    return lax.psum_scatter(once, "hi", scatter_dimension=0, tiled=False)


def row_tables(block_seq, block_len, core):
    blocks = SEQ_MAX // QLEN
    sequence, lengths = block_seq.reshape(blocks), block_len.reshape(blocks)
    index = jnp.arange(blocks, dtype=jnp.int32)
    same = sequence[:, None] == sequence[None, :]
    first = jnp.min(jnp.where(same, index[None, :], blocks), axis=1)
    table = jnp.stack([sequence, lengths, QLEN * (index - first)])
    turned = jnp.concatenate([table[:, blocks // 2 :], table[:, : blocks // 2]], axis=1)
    table = jnp.where(core == 0, table, turned)
    sequence, lengths, start = (jnp.repeat(part, QLEN)[:, None] for part in table)
    inside = (jnp.arange(SEQ_MAX, dtype=jnp.int32) % QLEN)[:, None]
    position = (start + inside).astype(f32)
    valid = inside < lengths

    lane = jnp.arange(SLOT, dtype=jnp.int32)
    half = HEAD_DIM // 2
    inverse = jnp.exp((lane % half).astype(f32) * (-2.0 * math.log(ROPE_BASE) / HEAD_DIM))
    angle = position * inverse[None, :]
    cosine = jnp.cos(angle)
    sine = jnp.sin(angle) * jnp.where(lane % HEAD_DIM < half, -1.0, 1.0)[None, :]

    column = (lane - HEAD_DIM)[None, :]
    in_mask = (column >= 0) & (column < blocks)
    match = column == sequence
    ext_q = jnp.where(in_mask & match, 1.0, 0.0).astype(bf16)
    ext_k = jnp.where(
        in_mask,
        jnp.where(match & valid, 0.0, MASKED),
        jnp.where((column >= 32) & (column < 35), -1.0, 0.0),
    ).astype(bf16)
    return cosine, sine, ext_q, ext_k


def local(
    split,
    axes,
    tokens,
    w_query,
    w_key,
    w_value,
    w_out,
    w_gate,
    w_up,
    w_down,
    attention_norm_gain,
    feedforward_norm_gain,
    block_seq,
    block_len,
    cotangent,
):
    depth, units = w_gate.shape
    mine = w_query.shape[1]
    pairs = mine // SLOT
    gain_a, gain_f = attention_norm_gain[None, :], feedforward_norm_gain[None, :]

    tokens_par = swap(tokens)
    qkv_shard = jnp.concatenate(
        [
            w[:, p * SLOT : (p + 1) * SLOT]
            for p in range(pairs)
            for w in (w_query, w_key, w_value)
        ],
        axis=1,
    )
    w_qkv = gather_rows(qkv_shard, split)
    at_up, at_down, at_out = units, 2 * units, 3 * units
    columns = at_out + mine
    w_rest = gather_rows(jnp.concatenate([w_gate, w_up, w_down.T, w_out.T], axis=1), split)
    cosine, sine, ext_q, ext_k = row_tables(block_seq, block_len, lax.axis_index("mp"))

    query, keys, values = project_qkv(tokens, tokens_par, w_qkv, cosine, sine, ext_q, ext_k)
    context, mixed, query = attend(query, keys, values)
    rows = tokens.shape[0]
    context_got = swap(context[rows:])
    out_other = swap(w_rest[:, at_out:])
    xhat_a, inverse_a, hidden = attention_out(
        context, context_got, w_rest, out_other, at_out, tokens, gain_a
    )
    hidden_par = swap(hidden)
    act, da, db = gate_up(hidden, w_rest, units)
    act_par, da_par, db_par = gate_up(hidden_par, w_rest, units)
    branch_got = swap(down(act_par, w_rest, at_down))
    output, middle, grad_branch, sum_f = down_norm(
        act, w_rest, at_down, branch_got, xhat_a, cotangent, gain_a, gain_f
    )

    grad_branch_par = swap(grad_branch)
    grad_gate, grad_up = gate_up_back(grad_branch, w_rest, at_down, da, db)
    grad_gate_par, grad_up_par = gate_up_back(grad_branch_par, w_rest, at_down, da_par, db_par)
    hidden_got = swap(hidden_back(grad_gate_par, grad_up_par, w_rest))
    tile = 512 if units % 512 == 0 else 128
    grads = weight_grad(
        split, grad_branch, grad_branch_par, act, act_par, 0, columns, at_down, tile
    )
    residual, grad_attn, grad_context, grad_context_send, sum_a = hidden_norm_back(
        grad_gate, grad_up, w_rest, hidden_got, middle, xhat_a, inverse_a, gain_a, at_out, out_other
    )
    grad_context_par = swap(grad_context_send)
    grad_attn_par = swap(grad_attn)
    grads = weight_grad(split, hidden, hidden_par, grad_gate, grad_gate_par, 0, columns, 0, tile, grads)
    grads = weight_grad(split, hidden, hidden_par, grad_up, grad_up_par, 0, columns, at_up, tile, grads)
    grads = weight_grad(
        split, grad_attn, grad_attn_par, context, context, 1, columns, at_out, mine, grads
    )
    grad_rest = scatter_rows(grads, split)
    gains = sum_everywhere(
        jnp.stack([jnp.sum(sum_a, axis=0), jnp.sum(sum_f, axis=0)]), axes
    )
    pieces = [
        attend_back(
            p, query, keys, values, grad_context, grad_context_par, mixed, cosine, sine
        )
        for p in range(pairs)
    ]
    input_got = swap(input_back(pieces, w_qkv, True))
    grads = None
    for p, piece in enumerate(pieces):
        grads = weight_grad(
            split, tokens, tokens_par, piece, piece, 1, 3 * mine, p * 3 * SLOT, 3 * SLOT, grads
        )
    grad_qkv = scatter_rows(grads, split)
    input_grad = input_back(pieces, w_qkv, False, (residual, input_got))

    grad_rest = grad_rest.astype(f32)
    grad_qkv = grad_qkv.astype(f32).reshape(depth, pairs, 3, SLOT)
    grad_query, grad_key, grad_value = (
        grad_qkv[:, :, n].reshape(depth, mine) for n in range(3)
    )
    return (
        output,
        input_grad,
        grad_query,
        grad_key,
        grad_value,
        grad_rest[:, at_out:].T,
        grad_rest[:, :at_up],
        grad_rest[:, at_up:at_down],
        grad_rest[:, at_down:at_out].T,
        gains[0],
        gains[1],
    )


def solution(mesh):
    n_dp, n_mp = mesh.shape["dp"], mesh.shape["mp"]
    inner = 4 if n_dp % 4 == 0 else 1
    outer = n_dp // inner
    fine = Mesh(mesh.devices.reshape(outer, inner, n_mp), ("hi", "lo", "mp"))
    dp = ("hi", "lo")
    rows = P(("hi", "lo", "mp"), None)
    axes = (("mp", n_mp), ("lo", inner), ("hi", outer))

    def layer(*operands):
        width = operands[0].shape[1]
        depth = width // n_dp
        split = (outer, inner) if depth % 16 == 0 and inner > 1 else None
        return jax.shard_map(
            functools.partial(local, split, axes),
            mesh=fine,
            in_specs=(
                rows,
                P(dp, "mp"),
                P(dp, "mp"),
                P(dp, "mp"),
                P("mp", dp),
                P(dp, "mp"),
                P(dp, "mp"),
                P("mp", dp),
                P(),
                P(),
                P(dp, None),
                P(dp, None),
                rows,
            ),
            out_specs=(
                rows,
                rows,
                P(dp, "mp"),
                P(dp, "mp"),
                P(dp, "mp"),
                P("mp", dp),
                P(dp, "mp"),
                P(dp, "mp"),
                P("mp", dp),
                P(),
                P(),
            ),
            check_vma=False,
        )(*operands)

    return layer
```

time: 2060 us -> 596 us (0.29)
  waiting for transfers between devices: 1080 us -> 229 us
  matrix products: 473 us -> 0 us
  Pallas kernels: 0 us -> 293 us
  blocking collectives: 211 us -> 0 us
  other arithmetic: 171 us -> 12.4 us
  local copies, waits for them, and re-layouts: 99.2 us -> 27 us
    dot_general x49 -> x0, matrix products: 473 us -> none  [the longest x8 90.6 us: one_block(): jnp.einsum('qhd,khd->hqk', query_block, key_pack, preferred_element_type=...]
    reduce_scatter x8 -> x2, waiting for transfers between devices: 499 us -> 27.6 us  [scatter_rows(): return lax.psum_scatter(once, 'hi', scatter_dimension=0, tiled=False)]
    unnamed x21 -> x8, waiting for transfers between devices: 389 us -> 79.9 us
    pallas_call x0 -> x23, Pallas kernels: none -> 293 us  [run(): pl.pallas_call(kernel, name=name, grid=grid, in_specs=in_specs, out_specs...]
    all_gather x4 -> x0, blocking collectives: 170 us -> none  [the longest x1 45.9 us: local(): lax.all_gather(w_query, 'dp', axis=0, tiled=True)]
    all_gather x7 -> x2, waiting for transfers between devices: 195 us -> 99.6 us  [gather_rows(): return lax.all_gather(shard, ('hi', 'lo'), axis=0, tiled=True)]
    convert_element_type x10 -> x4, other arithmetic: 98.3 us -> 4.52 us  [the longest x1 2.28 us: row_tables(): ext_k = jnp.where(in_mask, jnp.where(match & valid, 0.0, MASKED), jnp.whe...]
    dynamic_update_slice x8 -> x0, local copies, waits for them, and re-layouts: 67.5 us -> none  [one_pack(): lax.scan(one_block, (zeros, zeros), (query_pack, grad_pack, seq_pack.resh...]
  transfers between devices with their start and end apart: 18 -> 21, of which waited for: 16 -> 13; matrix products, arithmetic and copies ran while one was open for 4% -> 3% of each run, Pallas kernels for 0% -> 21%
where the time goes in v1:
time: 596 us; the launch traced here: 585 us
  Pallas kernels  293 us (49%)
  waiting for transfers between devices  229 us (38%)
  local copies, waits for them, and re-layouts  27 us (5%)
  between operations  14.8 us (2%)
  other arithmetic  12.4 us (2%)
  starting transfers between devices  9.48 us (2%)
    pallas_call x23, Pallas kernels, run(): pl.pallas_call(kernel, name=name, grid=grid, in_specs=in_specs, out_specs...  293 us
    all_gather x2, waiting for transfers between devices, gather_rows(): return lax.all_gather(shard, ('hi', 'lo'), axis=0, tiled=True)  99.6 us
    unnamed x8, waiting for transfers between devices  79.9 us
    reduce_scatter x2, waiting for transfers between devices, scatter_rows(): return lax.psum_scatter(once, 'hi', scatter_dimension=0, tiled=False)  27.6 us
    unnamed x49, local copies, waits for them, and re-layouts  18.4 us
  transfers between devices with their start and end apart: 21, of which 13 were waited for; matrix products, arithmetic and copies ran while one was open for 3% of the time, Pallas kernels for 21%

profile of v1, /device:TPU:0, one launch (start us, length us, event | category | flops | bytes accessed | tf_op | source)
XLA Modules:
  0.0 585.2 jit_solution(18442070096179651166)
XLA Ops:
  7.3 0.8 constant_dynamic-update-slice_fusion.8
  8.1 0.7 constant_dynamic-update-slice_fusion.7
  8.8 0.7 constant_dynamic-update-slice_fusion.6
  9.5 0.7 constant_dynamic-update-slice_fusion.5
  10.9 0.7 constant_dynamic-update-slice_fusion.3
  11.6 0.7 constant_dynamic-update-slice_fusion.2
  14.5 1.9 pad_maximum_fusion
  17.9 1.1 select_convert_fusion.1.eq_ref
  19.0 2.3 select_convert_fusion.ek_ref
  21.3 5.6 fusion
  26.9 49.3 %all-gather.3.cloned.1.call-done.w_ref.refs_3_ = bf16[768,1152]{1,0:T(8,128)(2,1)} async-done(((bf16[48,1152]{1,0:T(8,128)(2,1)}), bf16[768,1152]{1,0:T(8,128)(2,1)}) %all-gather.3.cloned.1.call-update) | async-done | bytes 1769488 | tf_op jit(solution)/shard_map/all_gather | solution.py:644
  76.3 12.9 %project_qkv.1 = (bf16[6,2048,128]{2,1,0:T(8,128)(2,1)}, bf16[6,2048,128]{2,1,0:T(8,128)(2,1)}, bf16[6,2048,128]{2,1,0:T(8,128)(2,1)}) custom-call(bf16[1024,768]{1,0:T(8,128)(2,1)} %own_ref.7, bf16[1024,768]{1,0:T(8,128)(2,1)} %copy-done.1, bf16[768,1152]{1,0:T(8,128)(2,1)} %all-gather.3.cloned.1.call-done.w_ref.refs_3_, ...), custom_call_target="tpu_custom_call" | custom-call | flops 3623878656 | bytes 17498112 | tf_op jit(solution)/shard_map/project_qkv/pallas_call | solution.py:35
  89.2 43.4 %attend.1 = (bf16[2048,384]{1,0:T(8,128)(2,1)}, f32[2048,384]{1,0:T(8,128)}, bf16[6,2048,128]{2,1,0:T(8,128)(2,1)}) custom-call(bf16[6,2048,128]{2,1,0:T(8,128)(2,1)} %get-tuple-element.39.q_ref, bf16[6,2048,128]{2,1,0:T(8,128)(2,1)} %get-tuple-element.40.k_ref, bf16[6,2048,128]{2,1,0:T(8,128)(2,1)} %get-tuple-element.41.v_ref), custom_call_target="tpu_custom_call" | custom-call | flops 12884901888 | bytes 17301504 | tf_op jit(solution)/shard_map/attend/pallas_call | solution.py:35
  132.6 1.2 slice.77
  133.9 50.3 %all-gather.5.cloned.1.call-done.mine_ref.gate_ref.up_ref.down_ref.wg_ref.wu_ref = bf16[768,4992]{1,0:T(8,128)(2,1)} async-done(((bf16[48,4992]{1,0:T(8,128)(2,1)}), bf16[768,4992]{1,0:T(8,128)(2,1)}) %all-gather.5.cloned.1.call-update) | async-done | bytes 7667728 | tf_op jit(solution)/shard_map/all_gather | solution.py:644
  184.2 1.1 slice.88
  186.0 1.4 collective-permute-done.2.other_ref
  187.4 0.8 copy-done.3
  188.2 6.9 %attention_out.1 = (f32[1024,768]{1,0:T(8,128)}, f32[1024,1]{1,0:T(8,128)}, bf16[1024,768]{1,0:T(8,128)(2,1)}) custom-call(bf16[2048,384]{1,0:T(8,128)(2,1)} %get-tuple-element.42.ctx_ref.yo_ref.yp_ref, bf16[1024,384]{1,0:T(8,128)(2,1)} %copy-done.10, bf16[768,4992]{1,0:T(8,128)(2,1)} %all-gather.5.cloned.1.call-done.mine_ref.gate_ref.up_ref.down_ref.wg_ref.wu_ref, ...), custom_call_target="tpu_custom_call" | custom-call | flops 1207959552 | bytes 16915456 | tf_op jit(solution)/shard_map/attention_out/pallas_call | solution.py:35
  195.3 3.5 collective-permute-done.3.x_ref.par_ref
  198.8 1.1 copy-done.2
  199.9 10.6 %gate_up.3 = (bf16[1024,1536]{1,0:T(8,128)(2,1)}, bf16[1024,1536]{1,0:T(8,128)(2,1)}, bf16[1024,1536]{1,0:T(8,128)(2,1)}) custom-call(bf16[1024,768]{1,0:T(8,128)(2,1)} %copy-done.2, bf16[768,4992]{1,0:T(8,128)(2,1)} %all-gather.5.cloned.1.call-done.mine_ref.gate_ref.up_ref.down_ref.wg_ref.wu_ref, ...), custom_call_target="tpu_custom_call" | custom-call | flops 4831838208 | bytes 26345472 | tf_op jit(solution)/shard_map/gate_up/pallas_call | solution.py:35
  210.5 6.5 %down.1 = bf16[1024,768]{1,0:T(8,128)(2,1)} custom-call(bf16[1024,1536]{1,0:T(8,128)(2,1)} %get-tuple-element.45.act_ref.yp_ref, bf16[768,4992]{1,0:T(8,128)(2,1)} %all-gather.5.cloned.1.call-done.mine_ref.gate_ref.up_ref.down_ref.wg_ref.wu_ref), custom_call_target="tpu_custom_call" | custom-call | flops 2415919104 | bytes 12386304 | tf_op jit(solution)/shard_map/down/pallas_call | solution.py:35
  217.6 10.5 %gate_up.2 = (bf16[1024,1536]{1,0:T(8,128)(2,1)}, bf16[1024,1536]{1,0:T(8,128)(2,1)}, bf16[1024,1536]{1,0:T(8,128)(2,1)}) custom-call(bf16[1024,768]{1,0:T(8,128)(2,1)} %get-tuple-element.43.x_ref.own_ref, bf16[768,4992]{1,0:T(8,128)(2,1)} %all-gather.5.cloned.1.call-done.mine_ref.gate_ref.up_ref.down_ref.wg_ref.wu_ref, ...), custom_call_target="tpu_custom_call" | custom-call | flops 4831838208 | bytes 26345472 | tf_op jit(solution)/shard_map/gate_up/pallas_call | solution.py:35
  228.2 1.2 copy-done.7
  229.4 10.0 %down_norm.1 = (bf16[1024,768]{1,0:T(8,128)(2,1)}, f32[1024,768]{1,0:T(8,128)}, bf16[1024,768]{1,0:T(8,128)(2,1)}, f32[8,768]{1,0:T(8,128)}) custom-call(bf16[1024,1536]{1,0:T(8,128)(2,1)} %get-tuple-element.44.act_ref.yo_ref, bf16[768,4992]{1,0:T(8,128)(2,1)} %all-gather.5.cloned.1.call-done.mine_ref.gate_ref.up_ref.down_ref.wg_ref.wu_ref, ...), custom_call_target="tpu_custom_call" | custom-call | flops 2415919104 | bytes 23427072 | tf_op jit(solution)/shard_map/down_norm/pallas_call | solution.py:35
  239.8 3.3 collective-permute-done.5.g_ref.par_ref
  243.1 1.2 copy-done.5
  244.2 9.7 %gate_up_back.3 = (bf16[1024,1536]{1,0:T(8,128)(2,1)}, bf16[1024,1536]{1,0:T(8,128)(2,1)}) custom-call(bf16[1024,768]{1,0:T(8,128)(2,1)} %copy-done.5, bf16[768,4992]{1,0:T(8,128)(2,1)} %all-gather.5.cloned.1.call-done.mine_ref.gate_ref.up_ref.down_ref.wg_ref.wu_ref, bf16[1024,1536]{1,0:T(8,128)(2,1)} %get-tuple-element.54.da_ref, ...), custom_call_target="tpu_custom_call" | custom-call | flops 2415919104 | bytes 21823488 | tf_op jit(solution)/shard_map/gate_up_back/pallas_call | solution.py:35
  253.9 9.5 %hidden_back.1 = bf16[1024,768]{1,0:T(8,128)(2,1)} custom-call(bf16[1024,1536]{1,0:T(8,128)(2,1)} %get-tuple-element.56.gate_ref.yp_ref, bf16[1024,1536]{1,0:T(8,128)(2,1)} %get-tuple-element.57.up_ref.yp_ref, bf16[768,4992]{1,0:T(8,128)(2,1)} %all-gather.5.cloned.1.call-done.mine_ref.gate_ref.up_ref.down_ref.wg_ref.wu_ref, ...), custom_call_target="tpu_custom_call" | custom-call | flops 4831838208 | bytes 23199744 | tf_op jit(solution)/shard_map/hidden_back/pallas_call | solution.py:35
  263.7 10.2 %gate_up_back.2 = (bf16[1024,1536]{1,0:T(8,128)(2,1)}, bf16[1024,1536]{1,0:T(8,128)(2,1)}) custom-call(bf16[1024,768]{1,0:T(8,128)(2,1)} %get-tuple-element.49.g_ref.own_ref, bf16[768,4992]{1,0:T(8,128)(2,1)} %all-gather.5.cloned.1.call-done.mine_ref.gate_ref.up_ref.down_ref.wg_ref.wu_ref, bf16[1024,1536]{1,0:T(8,128)(2,1)} %get-tuple-element.50.da_ref, ...), custom_call_target="tpu_custom_call" | custom-call | flops 2415919104 | bytes 21823488 | tf_op jit(solution)/shard_map/gate_up_back/pallas_call | solution.py:35
  273.9 1.1 copy-done.4
  275.1 17.5 %hidden_norm_back.1 = (f32[1024,768]{1,0:T(8,128)}, bf16[1024,768]{1,0:T(8,128)(2,1)}, bf16[1024,384]{1,0:T(8,128)(2,1)}, bf16[1024,384]{1,0:T(8,128)(2,1)}, f32[8,768]{1,0:T(8,128)}) custom-call(bf16[1024,1536]{1,0:T(8,128)(2,1)} %get-tuple-element.52.gate_ref.yo_ref, bf16[1024,1536]{1,0:T(8,128)(2,1)} %get-tuple-element.53.up_ref.yo_ref, ...), custom_call_target="tpu_custom_call" | custom-call | flops 6039797760 | bytes 44071936 | tf_op jit(solution)/shard_map/hidden_norm_back/pallas_call | solution.py:35
  292.7 2.3 collective-permute-done.7.par_ref
  295.1 0.9 copy-done.18
  296.0 27.0 %attend_back.5.refs_2_.yo_ref.yp_ref = bf16[2048,384]{1,0:T(8,128)(2,1)} custom-call(bf16[6,2048,128]{2,1,0:T(8,128)(2,1)} %get-tuple-element.48.q_ref, bf16[6,2048,128]{2,1,0:T(8,128)(2,1)} %get-tuple-element.40.k_ref, bf16[6,2048,128]{2,1,0:T(8,128)(2,1)} %get-tuple-element.41.v_ref, bf16[1024,384]{1,0:T(8,128)(2,1)} %get-tuple-element.60.own_ref, ...), custom_call_target="tpu_custom_call" | custom-call | flops 10737418240 | bytes 17825792 | tf_op jit(solution)/shard_map/attend_back/pallas_call | solution.py:35
  323.0 27.3 %attend_back.4.refs_1_.yo_ref.yp_ref = bf16[2048,384]{1,0:T(8,128)(2,1)} custom-call(bf16[6,2048,128]{2,1,0:T(8,128)(2,1)} %get-tuple-element.48.q_ref, bf16[6,2048,128]{2,1,0:T(8,128)(2,1)} %get-tuple-element.40.k_ref, bf16[6,2048,128]{2,1,0:T(8,128)(2,1)} %get-tuple-element.41.v_ref, bf16[1024,384]{1,0:T(8,128)(2,1)} %get-tuple-element.60.own_ref, ...), custom_call_target="tpu_custom_call" | custom-call | flops 10737418240 | bytes 17825792 | tf_op jit(solution)/shard_map/attend_back/pallas_call | solution.py:35
  350.3 27.3 %attend_back.3.refs_0_.yo_ref.yp_ref = bf16[2048,384]{1,0:T(8,128)(2,1)} custom-call(bf16[6,2048,128]{2,1,0:T(8,128)(2,1)} %get-tuple-element.48.q_ref, bf16[6,2048,128]{2,1,0:T(8,128)(2,1)} %get-tuple-element.40.k_ref, bf16[6,2048,128]{2,1,0:T(8,128)(2,1)} %get-tuple-element.41.v_ref, bf16[1024,384]{1,0:T(8,128)(2,1)} %get-tuple-element.60.own_ref, ...), custom_call_target="tpu_custom_call" | custom-call | flops 10737418240 | bytes 17825792 | tf_op jit(solution)/shard_map/attend_back/pallas_call | solution.py:35
  377.6 5.0 weight_grad.7.refs_0_
  382.6 5.0 weight_grad.8.refs_0_
  387.6 5.0 weight_grad.9
  392.7 1.3 copy-done.8
  394.2 10.1 %weight_grad.10.refs_0_ = bf16[4,4,48,4992]{3,2,1,0:T(8,128)(2,1)} custom-call(bf16[1024,768]{1,0:T(8,128)(2,1)} %get-tuple-element.49.g_ref.own_ref, bf16[1024,768]{1,0:T(8,128)(2,1)} %copy-done.5, bf16[1024,1536]{1,0:T(8,128)(2,1)} %get-tuple-element.44.act_ref.yo_ref, bf16[1024,1536]{1,0:T(8,128)(2,1)} %get-tuple-element.45.act_ref.yp_ref), custom_call_target="tpu_custom_call" | custom-call | flops 4831838208 | bytes 17104896 | tf_op jit(solution)/shard_map/weight_grad/pallas_call | solution.py:35
  404.3 10.0 %weight_grad.11.refs_0_ = bf16[4,4,48,4992]{3,2,1,0:T(8,128)(2,1)} custom-call(bf16[1024,768]{1,0:T(8,128)(2,1)} %get-tuple-element.43.x_ref.own_ref, bf16[1024,768]{1,0:T(8,128)(2,1)} %copy-done.2, bf16[1024,1536]{1,0:T(8,128)(2,1)} %get-tuple-element.52.gate_ref.yo_ref, ...), custom_call_target="tpu_custom_call", output_to_operand_aliasing={{}: (4, {})} | custom-call | flops 4831838208 | bytes 24772608 | tf_op jit(solution)/shard_map/weight_grad/pallas_call | solution.py:35
  414.3 10.2 %weight_grad.12.refs_0_ = bf16[4,4,48,4992]{3,2,1,0:T(8,128)(2,1)} custom-call(bf16[1024,768]{1,0:T(8,128)(2,1)} %get-tuple-element.43.x_ref.own_ref, bf16[1024,768]{1,0:T(8,128)(2,1)} %copy-done.2, bf16[1024,1536]{1,0:T(8,128)(2,1)} %get-tuple-element.53.up_ref.yo_ref, ...), custom_call_target="tpu_custom_call", output_to_operand_aliasing={{}: (4, {})} | custom-call | flops 4831838208 | bytes 24772608 | tf_op jit(solution)/shard_map/weight_grad/pallas_call | solution.py:35
  424.5 1.1 copy-done.9
  425.6 5.0 weight_grad.13
  431.2 79.3 %reduce-scatter.15.cloned.1.call-done = bf16[1,4,48,4992]{3,2,1,0:T(8,128)(2,1)} async-done(((bf16[4,4,48,4992]{3,2,1,0:T(8,128)(2,1)}), bf16[1,4,48,4992]{3,2,1,0:T(8,128)(2,1)}) %reduce-scatter.15.cloned.1.call-update) | async-done | bytes 1916944
  510.6 6.1 %input_back.2 = bf16[1024,768]{1,0:T(8,128)(2,1)} custom-call(bf16[2048,384]{1,0:T(8,128)(2,1)} %attend_back.3.refs_0_.yo_ref.yp_ref, bf16[2048,384]{1,0:T(8,128)(2,1)} %attend_back.4.refs_1_.yo_ref.yp_ref, bf16[2048,384]{1,0:T(8,128)(2,1)} %attend_back.5.refs_2_.yo_ref.yp_ref, bf16[768,1152]{1,0:T(8,128)(2,1)} %all-gather.3.cloned.1.call-done.w_ref.refs_3_), custom_call_target="tpu_custom_call" | custom-call | flops 1811939328 | bytes 8060928 | tf_op jit(solution)/shard_map/input_back/pallas_call | solution.py:35
  517.3 2.4 collective-permute-done.10
  519.7 1.4 collective-permute-start.11
  521.1 2.3 collective-permute-done.11
  523.5 1.3 collective-permute-start.12
  524.8 2.4 collective-permute-done.12
  527.2 1.5 collective-permute-start.13
  528.7 2.2 collective-permute-done.13
  530.8 2.4 collective-permute-start.14
  533.2 2.1 collective-permute-done.14
  536.0 1.1 copy-done.6
  537.1 7.0 %input_back.3 = bf16[1024,768]{1,0:T(8,128)(2,1)} custom-call(bf16[2048,384]{1,0:T(8,128)(2,1)} %attend_back.3.refs_0_.yo_ref.yp_ref, bf16[2048,384]{1,0:T(8,128)(2,1)} %attend_back.4.refs_1_.yo_ref.yp_ref, bf16[2048,384]{1,0:T(8,128)(2,1)} %attend_back.5.refs_2_.yo_ref.yp_ref, bf16[768,1152]{1,0:T(8,128)(2,1)} %all-gather.3.cloned.1.call-done.w_ref.refs_3_, ...), custom_call_target="tpu_custom_call" | custom-call | flops 1811939328 | bytes 12779520 | tf_op jit(solution)/shard_map/input_back/pallas_call | solution.py:35
  544.1 1.0 reshape.116
  547.6 27.6 %reduce-scatter.11.cloned.1.call-done = bf16[1,48,4992]{2,1,0:T(8,128)(2,1)} async-done(((bf16[4,48,4992]{2,1,0:T(8,128)(2,1)}), bf16[1,48,4992]{2,1,0:T(8,128)(2,1)}) %reduce-scatter.11.cloned.1.call-update) | async-done | bytes 479248 | tf_op jit(solution)/shard_map/reduce_scatter | solution.py:651
  575.3 1.1 bitcast_convert_fusion
  577.0 0.9 slice_bitcast_fusion
  (99 shorter events, 12.2 us)
Async XLA Ops:
  7.2 9.3 %copy-start = (bf16[1024,768]{1,0:T(8,128)(2,1)S(1)}, bf16[1024,768]{1,0:T(8,128)(2,1)}, u32[]{:S(2)}) copy-start(bf16[1024,768]{1,0:T(8,128)(2,1)} %own_ref.7) | copy-start | bytes 4718596
  7.2 9.8 %copy-start.16 = (s32[1,32]{1,0:T(1,128)S(1)}, s32[1,32]{1,0:T(1,128)}, u32[]{:S(2)}) copy-start(s32[1,32]{1,0:T(1,128)} %param.23) | copy-start | bytes 388
  7.2 10.0 %copy-start.17 = (s32[1,32]{1,0:T(1,128)S(1)}, s32[1,32]{1,0:T(1,128)}, u32[]{:S(2)}) copy-start(s32[1,32]{1,0:T(1,128)} %param.24) | copy-start | bytes 388
  7.2 69.0 %all-gather.3.cloned.1.call-start = ((), (), s32[]{:S(2)}) async-start(), calls=%async_computation.4 | async-start | bytes 1880064 | tf_op jit(solution)/shard_map/all_gather | solution.py:644
  13.8 0.6 copy-start.11
  14.5 169.7 %all-gather.5.cloned.1.call-start = ((), (), s32[]{:S(2)}) async-start(), calls=%async_computation.5 | async-start | bytes 8146944 | tf_op jit(solution)/shard_map/all_gather | solution.py:644
  16.4 414.3 %reduce-scatter.13.cloned.1.call-start = ((), (), s32[]{:S(2)}) async-start(), calls=%async_computation.8 | async-start | bytes 2211840
  16.5 10.4 %collective-permute-start = (bf16[1024,768]{1,0:T(8,128)(2,1)S(1)}, bf16[1024,768]{1,0:T(8,128)(2,1)S(1)}, u32[]{:S(2)}, u32[]{:S(2)}) collective-permute-start(bf16[1024,768]{1,0:T(8,128)(2,1)S(1)} %copy-done), channel_id=1, source_target_pairs={{0,1},{1,0},{2,3},{3,2},{4,5},{5,4},{6,7},{7,6},{8,9},{9,8},{10,11... | collective-permute-start | bytes 4718600 | tf_op jit(solution)/shard_map/ppermute | solution.py:626
  26.9 49.4 %copy-start.1 = (bf16[1024,768]{1,0:T(8,128)(2,1)}, bf16[1024,768]{1,0:T(8,128)(2,1)S(1)}, u32[]{:S(2)}) copy-start(bf16[1024,768]{1,0:T(8,128)(2,1)S(1)} %collective-permute-done.par_ref) | copy-start | bytes 4718596
  132.6 52.8 %copy-start.14 = (f32[768]{0:T(1024)S(1)}, f32[768]{0:T(1024)}, u32[]{:S(2)}) copy-start(f32[768]{0:T(1024)} %param.21) | copy-start | bytes 9220
  133.8 52.1 %collective-permute-start.1 = (bf16[1024,384]{1,0:T(8,128)(2,1)S(1)}, bf16[1024,384]{1,0:T(8,128)(2,1)S(1)}, u32[]{:S(2)}, u32[]{:S(2)}) collective-permute-start(bf16[1024,384]{1,0:T(8,128)(2,1)S(1)} %slice.77), channel_id=1, source_target_pairs={{0,1},{1,0},{2,3},{3,2},{4,5},{5,4},{6,7},{7,6},{8,9},{9,8},{10,11... | collective-permute-start | bytes 2359304 | tf_op jit(solution)/shard_map/ppermute | solution.py:626
  185.3 2.1 collective-permute-start.2
  186.0 1.4 copy-start.10
  187.4 0.8 copy-start.3
  195.1 3.6 collective-permute-start.3
  198.7 1.1 copy-start.2
  210.5 6.6 %copy-start.15 = (f32[768]{0:T(1024)S(1)}, f32[768]{0:T(1024)}, u32[]{:S(2)}) copy-start(f32[768]{0:T(1024)} %param.22) | copy-start | bytes 9220
  216.9 11.3 %collective-permute-start.4 = (bf16[1024,768]{1,0:T(8,128)(2,1)}, bf16[1024,768]{1,0:T(8,128)(2,1)S(1)}, u32[]{:S(2)}, u32[]{:S(2)}) collective-permute-start(bf16[1024,768]{1,0:T(8,128)(2,1)} %down.1), channel_id=1, source_target_pairs={{0,1},{1,0},{2,3},{3,2},{4,5},{5,4},{6,7},{7,6},{8,9},{9,8},{10,11... | collective-permute-start | bytes 4718600 | tf_op jit(solution)/shard_map/ppermute | solution.py:626
  228.2 1.2 copy-start.7
  239.4 3.7 collective-permute-start.5
  243.0 1.2 copy-start.5
  263.4 10.5 %collective-permute-start.6 = (bf16[1024,768]{1,0:T(8,128)(2,1)}, bf16[1024,768]{1,0:T(8,128)(2,1)S(1)}, u32[]{:S(2)}, u32[]{:S(2)}) collective-permute-start(bf16[1024,768]{1,0:T(8,128)(2,1)} %hidden_back.1), channel_id=1, source_target_pairs={{0,1},{1,0},{2,3},{3,2},{4,5},{5,4},{6,7},{7,6},{8,9},{9,8},{10,11... | collective-permute-start | bytes 4718600 | tf_op jit(solution)/shard_map/ppermute | solution.py:626
  273.9 1.1 copy-start.4
  292.5 2.6 collective-permute-start.7
  295.1 0.9 copy-start.18
  392.6 1.4 copy-start.8
  392.6 117.9 %reduce-scatter.15.cloned.1.call-start = ((), (), s32[]{:S(2)}) async-start(), calls=%async_computation.9 | async-start | bytes 9584640
  394.0 30.4 %collective-permute-start.9 = (bf16[1024,768]{1,0:T(8,128)(2,1)S(1)}, bf16[1024,768]{1,0:T(8,128)(2,1)S(1)}, u32[]{:S(2)}, u32[]{:S(2)}) collective-permute-start(bf16[1024,768]{1,0:T(8,128)(2,1)S(1)} %copy-done.8), channel_id=1, source_target_pairs={{0,1},{1,0},{2,3},{3,2},{4,5},{5,4},{6,7},{7,6},{8,9},{9,8},{10,11... | collective-permute-start | bytes 4718600 | tf_op jit(solution)/shard_map/ppermute | solution.py:626
  424.5 1.1 copy-start.9
  430.6 113.5 %reduce-scatter.9.cloned.1.call-start = ((), (), s32[]{:S(2)}) async-start(), calls=%async_computation.6 | async-start | bytes 552960 | tf_op jit(solution)/shard_map/reduce_scatter | solution.py:651
  431.2 144.1 %reduce-scatter.11.cloned.1.call-start = ((), (), s32[]{:S(2)}) async-start(), calls=%async_computation.7 | async-start | bytes 2396160 | tf_op jit(solution)/shard_map/reduce_scatter | solution.py:651
  510.6 6.1 %copy-start.12 = (f32[8,768]{1,0:T(8,128)S(1)}, f32[8,768]{1,0:T(8,128)}, u32[]{:S(2)}) copy-start(f32[8,768]{1,0:T(8,128)} %get-tuple-element.66) | copy-start | bytes 73732
  510.6 6.1 %copy-start.13 = (f32[8,768]{1,0:T(8,128)S(1)}, f32[8,768]{1,0:T(8,128)}, u32[]{:S(2)}) copy-start(f32[8,768]{1,0:T(8,128)} %get-tuple-element.65) | copy-start | bytes 73732
  516.7 19.3 %collective-permute-start.8 = (bf16[1024,768]{1,0:T(8,128)(2,1)}, bf16[1024,768]{1,0:T(8,128)(2,1)S(1)}, u32[]{:S(2)}, u32[]{:S(2)}) collective-permute-start(bf16[1024,768]{1,0:T(8,128)(2,1)} %input_back.2), channel_id=1, source_target_pairs={{0,1},{1,0},{2,3},{3,2},{4,5},{5,4},{6,7},{7,6},{8,9},{9,8},{10,11... | collective-permute-start | bytes 4718600 | tf_op jit(solution)/shard_map/ppermute | solution.py:626
  516.8 2.9 collective-permute-start.10
  519.7 3.7 collective-permute-start.11
  523.5 3.7 collective-permute-start.12
  527.2 3.6 collective-permute-start.13
  530.8 4.5 collective-permute-start.14
  536.0 1.1 copy-start.6
Sparse Core Ops, SparseCore 0:
  14.6 61.6 all-gather.2
  79.0 105.0 all-gather.4
  392.8 30.6 reduce-scatter.12
  430.7 79.7 reduce-scatter.14
  512.7 21.0 reduce-scatter.8
  536.1 39.1 reduce-scatter.10
